TPU v7x, 32 devices: a whole 2x2x4 slice. The times are simulated.
32 devices in a mesh: gx: 8 (over z, x), gy: 4 (over y, core).
Axes of the slice: x: 2, y: 2, z: 4, core: 2. Of those that a mesh axis runs over, the one named last changes fastest.
Arguments:
- increment: bfloat16 [64, 384, 512], P(None, 'gx', 'gy'), may hold values from -6 to 6
- ensemble: bfloat16 [4, 64, 384, 512], P(None, None, 'gx', 'gy'), may hold values from -6 to 6
- wind_u: bfloat16 [64, 384, 512], P(None, 'gx', 'gy'), may hold values from -0.94921875 to 0.94921875
- wind_v: bfloat16 [64, 384, 512], P(None, 'gx', 'gy'), may hold values from -0.94921875 to 0.94921875
- filter_length: float32 [64], replicated, may hold values from 8 to 3072
- jacobian: bfloat16 [32, 512, 64], P(('gx', 'gy')), may hold values from -0.75 to 0.75
- obs_weight: float32 [32, 512], P(('gx', 'gy')), may hold values from 0.1 to 1
- departure: bfloat16 [2048, 512, 128], P(('gx', 'gy')), may hold values from -6 to 6
- obs_home: int32 [2048], P(('gx', 'gy')), may hold values from 0 to 31, as said below
- obs_line: int32 [2048], P(('gx', 'gy')), may hold values from 0 to 47
- obs_count: int32 [2048], P(('gx', 'gy')), may hold values from 1 to 128
Outputs:
- grad_alpha: float32 [4, 64, 384, 512], P(None, None, 'gx', 'gy')
- grad_static: float32 [64, 384, 512], P(None, 'gx', 'gy')
Inputs may be any that keep to these rules, and one draw needn't show every extreme that they name: `obs_home`: the records of one device name 32 distinct grid devices, each exactly 2 times.
All inputs are finite; a program needn't handle non-finite values.
Results may differ from a plain program's by a relative error of at most 0.003.
Values may be sent and summed in bfloat16 or wider, within the bound.
A program may use at most 192 MiB of HBM per device.

v0:
```python
import functools
import jax
import jax.numpy as jnp
from jax import lax
from jax.experimental import pallas as pl
from jax.experimental.pallas import tpu as pltpu
from jax.sharding import PartitionSpec as P

HALO = 3
STRIP = 4
EDGE = 8
CODE = 32767.0
highest = lax.Precision.HIGHEST


def peer_id(axes, index):
    if len(axes) == 1:
        return {axes[0]: index}
    minor = lax.axis_size(axes[1])
    return {axes[0]: index // minor, axes[1]: index % minor}


def gather_kernel(axes, scatter, x_ref, o_ref, send_sem, recv_sem, own_sem):
    count = lax.axis_size(axes)
    me = lax.axis_index(axes[0])
    for name in axes[1:]:
        me = me * lax.axis_size(name) + lax.axis_index(name)
    barrier = pltpu.get_barrier_semaphore()

    def greet(k, _):
        pl.semaphore_signal(
            barrier,
            inc=1,
            device_id=peer_id(axes, lax.rem(me + k, count)),
            device_id_type=pl.DeviceIdType.MESH,
        )
        return 0

    lax.fori_loop(1, count, greet, 0)
    own = pltpu.make_async_copy(x_ref.at[me] if scatter else x_ref, o_ref.at[me], own_sem)
    own.start()
    pl.semaphore_wait(barrier, count - 1)

    def copy(k, slot):
        to = lax.rem(me + k, count)
        return pltpu.make_async_remote_copy(
            src_ref=x_ref.at[to] if scatter else x_ref,
            dst_ref=o_ref.at[slot],
            send_sem=send_sem.at[k],
            recv_sem=recv_sem.at[k],
            device_id=peer_id(axes, to),
            device_id_type=pl.DeviceIdType.MESH,
        )

    def send(k, _):
        copy(k, me).start()
        return 0

    def finish(k, _):
        landed = copy(k, lax.rem(me + count - k, count))
        landed.wait_send()
        landed.wait_recv()
        return 0

    lax.fori_loop(1, count, send, 0)
    own.wait()
    lax.fori_loop(1, count, finish, 0)


def exchange(x, axes, collective_id, scatter):
    count = lax.axis_size(axes)
    shape = x.shape if scatter else (count,) + x.shape
    return pl.pallas_call(
        functools.partial(gather_kernel, axes, scatter),
        out_shape=jax.ShapeDtypeStruct(shape, x.dtype),
        in_specs=[pl.BlockSpec(memory_space=pltpu.VMEM)],
        out_specs=pl.BlockSpec(memory_space=pltpu.VMEM),
        scratch_shapes=[
            pltpu.SemaphoreType.DMA((count,)),
            pltpu.SemaphoreType.DMA((count,)),
            pltpu.SemaphoreType.DMA,
        ],
        compiler_params=pltpu.CompilerParams(
            collective_id=collective_id, has_side_effects=True
        ),
        name="exchange_%d" % collective_id,
    )(x)


def split(value):
    high = value.astype(jnp.bfloat16)
    return high, (value - high.astype(jnp.float32)).astype(jnp.bfloat16)


def position(axes):
    me = lax.axis_index(axes[0])
    for name in axes[1:]:
        me = me * lax.axis_size(name) + lax.axis_index(name)
    return me


def coded(value):
    top = jnp.max(jnp.max(jnp.abs(value), axis=1, keepdims=True), axis=0, keepdims=True)
    top = jnp.maximum(top, 1e-30)
    code = jnp.round(value * (CODE / top)).astype(jnp.int32).astype(jnp.int16)
    return code, top * (1.0 / CODE)


def obs_kernel(
    axes, most, order_ref, line_ref, count_ref, j_ref, w_ref, d_hbm, got_ref, note_ref,
    d_buf, send_buf, note_buf, lhs_ref, hold_ref, scale_ref,
    d_sem, send_sem, recv_sem, note_send, note_recv,
):
    count = lax.axis_size(axes)
    half = count // 2
    me = position(axes)
    lev = j_ref.shape[1]
    cy = d_buf.shape[2]
    barrier = pltpu.get_barrier_semaphore()
    pieces = d_sem.shape[0]
    size = d_buf.shape[0] // pieces

    def piece(i):
        rows = pl.ds(i * size, size)
        return pltpu.make_async_copy(d_hbm.at[rows], d_buf.at[rows], d_sem.at[i])

    for i in range(pieces):
        piece(i).start()

    def greet(k, _):
        pl.semaphore_signal(
            barrier,
            inc=1,
            device_id=peer_id(axes, lax.rem(me + k, count)),
            device_id_type=pl.DeviceIdType.MESH,
        )
        return 0

    lax.fori_loop(1, count, greet, 0)
    turned = j_ref[...].astype(jnp.float32).T
    high, low = split(turned * w_ref[...])
    lhs_ref[...] = jnp.concatenate([high, low], axis=0)
    both = jnp.dot(lhs_ref[...], j_ref[...], preferred_element_type=jnp.float32)
    normal = both[:lev] + both[lev:]
    code, scale = coded(normal)
    hold_ref[...] = jnp.concatenate([code[: lev // 2], code[lev // 2 :]], axis=1)
    scale_ref[...] = jnp.broadcast_to(scale, scale_ref.shape)
    for i in range(pieces):
        piece(i).wait()
    pl.semaphore_wait(barrier, count - 1)
    lane = lax.broadcasted_iota(jnp.int32, (1, cy), 1)

    def fill(home, target, note):
        blocks = [d_buf[order_ref[home * most + m]] for m in range(most)]
        both = jnp.dot(
            lhs_ref[...], jnp.concatenate(blocks, axis=1), preferred_element_type=jnp.float32
        )
        word = jnp.where(lane == 3 * most, scale_ref[0:1, :], 0.0)
        for m in range(most):
            part = both[:lev, m * cy : (m + 1) * cy] + both[lev:, m * cy : (m + 1) * cy]
            code, scale = coded(part)
            target[m * lev : (m + 1) * lev, :] = code
            word = jnp.where(lane == m, line_ref[home * most + m].astype(jnp.float32), word)
            word = jnp.where(lane == most + m, count_ref[home * most + m].astype(jnp.float32), word)
            word = jnp.where(lane == 2 * most + m, scale, word)
        target[most * lev :, :] = hold_ref[...]
        note[...] = word

    def goal(t):
        j = t + t // half
        mine, place = me // half, lax.rem(me, half)
        other = lax.rem(mine + 1 + j // half, 2)
        return other * half + lax.rem(place + j, half)

    def sends(to, origin):
        peer = dict(device_id=peer_id(axes, to), device_id_type=pl.DeviceIdType.MESH)
        return (
            pltpu.make_async_remote_copy(
                src_ref=send_buf.at[to], dst_ref=got_ref.at[origin],
                send_sem=send_sem.at[to], recv_sem=recv_sem.at[origin], **peer
            ),
            pltpu.make_async_remote_copy(
                src_ref=note_buf.at[to], dst_ref=note_ref.at[origin],
                send_sem=note_send.at[to], recv_sem=note_recv.at[origin], **peer
            ),
        )

    def begin(to):
        for copy in sends(to, me):
            copy.start()

    first = goal(0)
    fill(first, send_buf.at[first], note_buf.at[first])

    def step(t, _):
        to = goal(t)
        fill(to, send_buf.at[to], note_buf.at[to])
        begin(goal(t - 1))
        return 0

    lax.fori_loop(1, count - 1, step, 0)
    fill(me, got_ref.at[me], note_ref.at[me])
    begin(goal(count - 2))

    def finish(k, _):
        peer = lax.rem(me + k, count)
        for copy in sends(peer, peer):
            copy.wait_send()
            copy.wait_recv()
        return 0

    lax.fori_loop(1, count, finish, 0)


def observe(order, lines, counts, jacobian, weight, departure, axes, most, collective_id):
    count = lax.axis_size(axes)
    channels, lev = jacobian.shape
    records, _, cy = departure.shape
    rows = most * lev + lev // 2
    smem = pl.BlockSpec(memory_space=pltpu.SMEM)
    vmem = pl.BlockSpec(memory_space=pltpu.VMEM)
    dma = pltpu.SemaphoreType.DMA
    return pl.pallas_call(
        functools.partial(obs_kernel, axes, most),
        out_shape=[
            jax.ShapeDtypeStruct((count, rows, cy), jnp.int16),
            jax.ShapeDtypeStruct((count, 1, cy), jnp.float32),
        ],
        in_specs=[smem, smem, smem, vmem, vmem, pl.BlockSpec(memory_space=pl.ANY)],
        out_specs=[vmem, vmem],
        scratch_shapes=[
            pltpu.VMEM((records, channels, cy), jnp.bfloat16),
            pltpu.VMEM((count, rows, cy), jnp.int16),
            pltpu.VMEM((count, 1, cy), jnp.float32),
            pltpu.VMEM((2 * lev, channels), jnp.bfloat16),
            pltpu.VMEM((lev // 2, 2 * lev), jnp.int16),
            pltpu.VMEM((8, cy), jnp.float32),
            dma((8,)), dma((count,)), dma((count,)), dma((count,)), dma((count,)),
        ],
        compiler_params=pltpu.CompilerParams(
            collective_id=collective_id,
            has_side_effects=True,
            vmem_limit_bytes=56 * 1024 * 1024,
        ),
        name="observe",
    )(order, lines, counts, jacobian, weight, departure)


def home_sums(most, note_ref, got_ref, c_ref, sum_ref):
    homes = got_ref.shape[0]
    lev, cy = c_ref.shape[1:]
    sum_ref[...] = jnp.zeros(sum_ref.shape, sum_ref.dtype)
    lane = lax.broadcasted_iota(jnp.int32, (lev // 2, 2 * lev), 1)
    column = lax.broadcasted_iota(jnp.int32, (lev, cy), 1)

    def one(k, _):
        code = got_ref[k, most * lev :, :].astype(jnp.int32).astype(jnp.float32)
        high, low = split(code)
        high, low = high.astype(jnp.float32), low.astype(jnp.float32)
        matrix = jnp.concatenate(
            [
                jnp.where(lane < lev, high, pltpu.roll(low, lev, 1)),
                jnp.where(lane < lev, pltpu.roll(high, lev, 1), low),
            ],
            axis=0,
        ).astype(jnp.bfloat16)
        lines = [note_ref[k, 0, m].astype(jnp.int32) for m in range(most)]
        block = jnp.concatenate([c_ref[line] for line in lines], axis=1)
        product = jnp.dot(
            matrix, jnp.concatenate([block, block], axis=0), preferred_element_type=jnp.float32
        )
        for m in range(most):
            part = got_ref[k, m * lev : (m + 1) * lev, :].astype(jnp.int32).astype(jnp.float32)
            value = (
                note_ref[k, 0, 3 * most] * product[:, m * cy : (m + 1) * cy]
                - note_ref[k, 0, 2 * most + m] * part
            )
            value = jnp.where(column < note_ref[k, 0, most + m].astype(jnp.int32), value, 0.0)
            rows = pl.ds(pl.multiple_of(lines[m] * lev, lev), lev)
            sum_ref[rows, :] += value
        return 0

    lax.fori_loop(0, homes, one, 0)


def ways():
    return [(dx, dy) for dx in (-1, 0, 1) for dy in (-1, 0, 1) if (dx, dy) != (0, 0)]


def halo_kernel(low_x, high_x, low_y, high_y, from_x, from_y, send_sem, recv_sem):
    gx, gy = lax.axis_index("gx"), lax.axis_index("gy")
    size_x, size_y = lax.axis_size("gx"), lax.axis_size("gy")
    barrier = pltpu.get_barrier_semaphore()

    def present(dx, dy):
        x, y = gx + dx, gy + dy
        return (x >= 0) & (x < size_x) & (y >= 0) & (y < size_y)

    def copy(k, dx, dy):
        if dy == 0:
            source = high_x if dx == 1 else low_x
            target = from_x.at[0 if dx == 1 else 1]
        else:
            source = high_y if dy == 1 else low_y
            target = from_y.at[1 - dx, 0 if dy == 1 else 1]
        return pltpu.make_async_remote_copy(
            src_ref=source,
            dst_ref=target,
            send_sem=send_sem.at[k],
            recv_sem=recv_sem.at[k],
            device_id={"gx": gx + dx, "gy": gy + dy},
            device_id_type=pl.DeviceIdType.MESH,
        )

    around = 0
    for dx, dy in ways():
        around = around + present(dx, dy).astype(jnp.int32)

        @pl.when(present(dx, dy))
        def _():
            pl.semaphore_signal(
                barrier,
                inc=1,
                device_id={"gx": gx + dx, "gy": gy + dy},
                device_id_type=pl.DeviceIdType.MESH,
            )

    pl.semaphore_wait(barrier, around)
    for k, (dx, dy) in enumerate(ways()):

        @pl.when(present(dx, dy))
        def _():
            copy(k, dx, dy).start()

    for k, (dx, dy) in enumerate(ways()):

        @pl.when(jnp.logical_not(present(-dx, -dy)))
        def _():
            if dy == 0:
                slot = 0 if dx == 1 else 1
                from_x[slot] = jnp.zeros(from_x.shape[1:], from_x.dtype)
            else:
                slot = 0 if dy == 1 else 1
                from_y[1 - dx, slot] = jnp.zeros(from_y.shape[2:], from_y.dtype)

    for k, (dx, dy) in enumerate(ways()):

        @pl.when(present(dx, dy))
        def _():
            copy(k, dx, dy).wait_send()

        @pl.when(present(-dx, -dy))
        def _():
            copy(k, dx, dy).wait_recv()


def halo(low_x, high_x, low_y, high_y, collective_id):
    return pl.pallas_call(
        halo_kernel,
        out_shape=[
            jax.ShapeDtypeStruct((2,) + low_x.shape, low_x.dtype),
            jax.ShapeDtypeStruct((3, 2) + low_y.shape, low_y.dtype),
        ],
        in_specs=[pl.BlockSpec(memory_space=pltpu.VMEM)] * 4,
        out_specs=[pl.BlockSpec(memory_space=pltpu.VMEM)] * 2,
        scratch_shapes=[pltpu.SemaphoreType.DMA((8,)), pltpu.SemaphoreType.DMA((8,))],
        compiler_params=pltpu.CompilerParams(
            collective_id=collective_id, has_side_effects=True
        ),
        name="halo",
    )(low_x, high_x, low_y, high_y)


def edge_columns(cy, width):
    row = lax.broadcasted_iota(jnp.int32, (2 * width, cy), 0)
    col = lax.broadcasted_iota(jnp.int32, (2 * width, cy), 1)
    return (col == jnp.where(row < width, row, row + cy - 2 * width)).astype(jnp.bfloat16)


def local_kernel(
    members, most, note_ref, got_ref, c_ref, e_ref, mx_ref, wy_ref,
    x_ref, sx_ref, sy_ref, rows_ref, sum_ref,
):
    _, levels, cx, cy = e_ref.shape
    lev = c_ref.shape[1]

    @pl.when(pl.program_id(0) == 0)
    def _():
        home_sums(most, note_ref, got_ref, c_ref, sum_ref)

    for l in range(levels):
        base = sum_ref[pl.ds(pl.program_id(0) * levels + l, cx, stride=lev), :]
        parts = [base] + [e_ref[m, l].astype(jnp.float32) * base for m in range(members)]
        high, low = split(jnp.concatenate(parts, axis=1))
        result = jnp.dot(
            mx_ref[l],
            jnp.concatenate([high, high, low], axis=0),
            preferred_element_type=jnp.float32,
        )
        stack = jnp.concatenate(
            [result[:cx, m * cy : (m + 1) * cy] for m in range(members + 1)], axis=0
        )
        x_ref[l] = stack
        for m in range(members + 1):
            rows_ref[m, l : l + 1, :] = result[cx : cx + 1, m * cy : (m + 1) * cy]
            rows_ref[members + 1 + m, l : l + 1, :] = result[0:1, m * cy : (m + 1) * cy]
        high, low = split(stack)
        sums = lax.dot_general(
            wy_ref[l],
            jnp.concatenate([high, low], axis=1),
            (((1,), (1,)), ((), ())),
            preferred_element_type=jnp.float32,
        )
        sy_ref[l] = sums[0:8] + sums[8:16]
    sx_ref[...] = rows_ref[...].astype(sx_ref.dtype)


def final_kernel(
    members, x_ref, ux_ref, ex_ref, my_ref, uy_ref, ey_ref, u_ref, v_ref,
    a_ref, s_ref, low_x, high_x, low_y, high_y,
):
    levels = x_ref.shape[0]
    _, _, cx, cy = a_ref.shape
    first = (((0,), (0,)), ((), ()))
    columns = edge_columns(cy, STRIP)
    for l in range(levels):
        field = x_ref[l] + lax.dot_general(
            ux_ref[l], ex_ref[l], first, preferred_element_type=jnp.float32
        )
        high, low = split(field)
        m_high, m_low = split(my_ref[l])
        weights = jnp.concatenate(
            [
                jnp.concatenate([m_high, m_low], axis=1),
                jnp.concatenate([m_high, jnp.zeros_like(m_low)], axis=1),
            ],
            axis=0,
        )
        both = jnp.dot(
            jnp.concatenate([high, low], axis=1), weights, preferred_element_type=jnp.float32
        )
        field = (
            both[:, :cy]
            + both[:, cy:]
            + lax.dot_general(ey_ref[l], uy_ref[l], first, preferred_element_type=jnp.float32)
        )
        static = field[:cx]
        s_ref[l] = static
        for m in range(members):
            a_ref[m, l] = field[(m + 1) * cx : (m + 2) * cx]
        for k, value in enumerate((static.astype(jnp.bfloat16), u_ref[l], v_ref[l])):
            low_x[k, l] = value[:STRIP]
            high_x[k, l] = value[cx - STRIP :]
            sides = lax.dot_general(
                columns, value, (((1,), (1,)), ((), ())), preferred_element_type=jnp.float32
            )
            low_y[k, l] = sides[:STRIP].astype(low_y.dtype)
            high_y[k, l] = sides[STRIP:].astype(high_y.dtype)


def transport_kernel(s_ref, u_ref, v_ref, hx_ref, hy_ref, o_ref):
    levels, cx, cy = o_ref.shape
    rows, lanes = cx + 2 * EDGE, 2 * cy
    blank = jnp.zeros((EDGE - STRIP, cy), jnp.float32)
    place = edge_columns(cy, STRIP)

    def widened(value, k, l):
        strips = []
        for j in range(3):
            pair = jnp.concatenate(
                [
                    hy_ref[j, 1, k, l].astype(jnp.float32),
                    hy_ref[j, 0, k, l].astype(jnp.float32),
                ],
                axis=0,
            ).astype(jnp.bfloat16)
            strips.append(
                lax.dot_general(
                    pair, place, (((0,), (0,)), ((), ())), preferred_element_type=jnp.float32
                )
            )
        above = hx_ref[0, k, l].astype(jnp.float32)
        below = hx_ref[1, k, l].astype(jnp.float32)
        return jnp.concatenate(
            [
                jnp.concatenate([blank, above, value, below, blank], axis=0),
                jnp.concatenate([strips[0][cx - EDGE :], strips[1], strips[2][:EDGE]], axis=0),
            ],
            axis=1,
        )

    for l in range(levels):
        s = widened(s_ref[l], 0, l)
        u = widened(u_ref[l].astype(jnp.float32), 1, l)
        v = widened(v_ref[l].astype(jnp.float32), 2, l)
        east, north = u > 0.0, v > 0.0
        u, v = jnp.abs(u), jnp.abs(v)
        for _ in range(HALO):
            s = s + u * (jnp.where(east, pltpu.roll(s, 1, 0), pltpu.roll(s, rows - 1, 0)) - s)
            s = s + v * (jnp.where(north, pltpu.roll(s, 1, 1), pltpu.roll(s, lanes - 1, 1)) - s)
        o_ref[l] = s[EDGE : EDGE + cx, :cy]


def smoother(lengths, count):
    pos = jnp.arange(count, dtype=jnp.float32)
    far = jnp.abs(pos[:, None] - pos[None, :])
    left = count - jnp.maximum(pos[:, None], pos[None, :])
    lengths = lengths[:, None, None]
    scale = -jnp.expm1(-1.0 / lengths) / jnp.sqrt(-jnp.expm1(-2.0 / lengths))
    return scale * jnp.exp(-far[None] / lengths) * -jnp.expm1(-2.0 * left[None] / lengths)


def end_weights(lengths, count):
    pos = jnp.arange(count, dtype=jnp.float32)
    coef = jnp.sqrt(-jnp.expm1(-2.0 / lengths))
    return coef[:, None] * jnp.exp(-(count - 1.0 - pos)[None, :] / lengths[:, None])


def responses(lengths, count):
    pos = jnp.arange(count, dtype=jnp.float32)[None, :]
    lengths = lengths[:, None]
    coef = -jnp.expm1(-1.0 / lengths)
    ratio = jnp.expm1(-2.0 * (count - pos) / lengths) / jnp.expm1(-2.0 / lengths)
    ahead = coef * jnp.exp(-(pos + 1.0) / lengths) * ratio
    behind = jnp.exp(-(count - pos) / lengths)
    return ahead, behind


def combine_weights(lengths, count, size, me):
    link = responses(lengths, count)[0][:, 0]
    k = jnp.arange(size)

    def power(steps, ok):
        return jnp.where(
            ok[..., None],
            jnp.exp(-jnp.maximum(steps, 0)[..., None] * (count / lengths)),
            0.0,
        )

    ahead = power(me - 1 - k, k < me)
    behind = power(k - me - 1, k > me)
    pair = power(k[:, None] - 1 - k[None, :], k[None, :] < k[:, None])
    cross = link[None, :] * jnp.sum(behind[:, None, :] * pair, axis=0)
    return ahead, behind, cross


def two_parts(value):
    high = lax.reduce_precision(value, 8, 7)
    return high, value - high


def whole_tiles(parts):
    joined = jnp.concatenate(parts, axis=1)
    return jnp.pad(joined, ((0, 0), (0, -joined.shape[1] % 16), (0, 0))).astype(jnp.bfloat16)


def left_terms(value):
    high, low = two_parts(value)
    return whole_tiles([high, low, high])


def right_terms(value):
    high, low = two_parts(value)
    return whole_tiles([high, high, low])


def body(
    increment,
    ensemble,
    wind_u,
    wind_v,
    filter_length,
    jacobian,
    obs_weight,
    departure,
    obs_home,
    obs_line,
    obs_count,
):
    axes = ("gx", "gy")
    home_count = lax.axis_size(axes)
    records_here = obs_home.shape[0]
    most = (records_here + home_count - 1) // home_count
    lev, cx, cy = increment.shape
    members = ensemble.shape[0]
    fields = members + 1
    slot_count = home_count * most
    index = jnp.arange(records_here, dtype=jnp.int32)
    earlier = (obs_home[:, None] == obs_home[None, :]) & (index[None, :] < index[:, None])
    slot_of = obs_home * most + jnp.sum(earlier.astype(jnp.int32), axis=1)
    placing = slot_of[:, None] == jnp.arange(slot_count, dtype=jnp.int32)[None, :]
    order, lines, counts = [
        jnp.sum(jnp.where(placing, value[:, None], 0), axis=0)
        for value in (index, obs_line, obs_count)
    ]
    got, note = observe(
        order, lines, counts, jacobian[0], obs_weight, departure, axes, most, 3
    )
    smooth_x = smoother(filter_length, cx)
    rows_x = jnp.concatenate(
        [
            smooth_x,
            end_weights(filter_length, cx)[:, None, :],
            jnp.zeros((lev, EDGE - 1, cx), jnp.float32),
        ],
        axis=1,
    )
    high_x = lax.reduce_precision(rows_x, 8, 7)
    cat_x = jnp.concatenate([high_x, rows_x - high_x, high_x], axis=2).astype(jnp.bfloat16)
    smooth_y = smoother(filter_length, cy)
    sums_y = jnp.stack([end_weights(filter_length, cy), smooth_y[:, 0, :]], axis=1)
    high_y = lax.reduce_precision(sums_y, 8, 7)
    low_y = sums_y - high_y
    blank = jnp.zeros((lev, 6, 2 * cy), jnp.float32)
    cat_y = jnp.concatenate(
        [
            jnp.concatenate([high_y, high_y], axis=2),
            blank,
            jnp.concatenate([low_y, jnp.zeros_like(low_y)], axis=2),
            blank,
        ],
        axis=1,
    ).astype(jnp.bfloat16)

    out_x = jnp.stack(responses(filter_length, cx), axis=0)
    same = jnp.eye(fields, dtype=jnp.float32)
    block_x = left_terms(
        (
            jnp.moveaxis(out_x, 0, 1)[:, :, None, None, :] * same[None, None, :, :, None]
        ).reshape(lev, 2 * fields, fields * cx)
    )
    out_y = right_terms(jnp.stack(responses(filter_length, cy), axis=1))
    across = jnp.transpose(increment, (1, 0, 2))
    tile = 16
    steps = lev // tile
    def levels_first(*shape):
        return pl.BlockSpec((tile,) + shape, lambda i: (i, 0, 0))

    params = pltpu.CompilerParams(
        dimension_semantics=("arbitrary",), vmem_limit_bytes=56 * 1024 * 1024
    )
    local, state_x, state_y = pl.pallas_call(
        functools.partial(local_kernel, members, most),
        grid=(steps,),
        in_specs=[
            pl.BlockSpec(memory_space=pltpu.SMEM),
            pl.BlockSpec(got.shape, lambda i: (0, 0, 0), pipeline_mode=pl.Buffered(1)),
            pl.BlockSpec(across.shape, lambda i: (0, 0, 0), pipeline_mode=pl.Buffered(1)),
            pl.BlockSpec((members, tile, cx, cy), lambda i: (0, i, 0, 0)),
            levels_first(cx + EDGE, 3 * cx),
            levels_first(16, 2 * cy),
        ],
        out_specs=[
            levels_first(fields * cx, cy),
            pl.BlockSpec((2 * fields, tile, cy), lambda i: (0, i, 0)),
            levels_first(8, fields * cx),
        ],
        out_shape=[
            jax.ShapeDtypeStruct((lev, fields * cx, cy), jnp.float32),
            jax.ShapeDtypeStruct((2 * fields, lev, cy), jnp.bfloat16),
            jax.ShapeDtypeStruct((lev, 8, fields * cx), jnp.float32),
        ],
        scratch_shapes=[
            pltpu.VMEM((2 * fields, tile, cy), jnp.float32),
            pltpu.VMEM((cx * lev, cy), jnp.float32),
        ],
        compiler_params=params,
        name="local",
    )(note, got, across, ensemble, cat_x, cat_y)

    size_x = lax.axis_size("gx")
    part = lev // size_x
    own = lax.axis_index("gx") * part
    mine = lax.dynamic_slice_in_dim(filter_length, own, part, 0)
    sent = jnp.moveaxis(state_x.reshape(2 * fields, size_x, part, cy), 1, 0)
    all_x = exchange(sent, ("gx",), 1, True).astype(jnp.float32)
    ahead, behind, cross = [
        jnp.stack(w) for w in zip(*[combine_weights(mine, cx, size_x, d) for d in range(size_x)])
    ]
    front, back = all_x[:, :fields], all_x[:, fields:]
    enter_x = sum(ahead[:, k, None, :, None] * front[k][None] for k in range(size_x))
    leave_x = sum(
        behind[:, k, None, :, None] * back[k][None] + cross[:, k, None, :, None] * front[k][None]
        for k in range(size_x)
    )
    swept = jnp.concatenate([enter_x, leave_x], axis=1).astype(jnp.bfloat16)
    swept = exchange(swept, ("gx",), 4, True).astype(jnp.float32)
    swept = jnp.moveaxis(swept, 0, 1).reshape(2, fields, lev, cy)
    enter_x, leave_x = swept[0], swept[1]
    edges_x = jnp.stack([enter_x, leave_x], axis=0)
    extra = jnp.sum(
        edges_x[:, :, :, None, :] * jnp.moveaxis(sums_y, 1, 1)[None, None], axis=-1
    )
    state_y = jnp.moveaxis(state_y[:, :2], 1, 0).reshape(2, lev, fields, cx) + sum(
        jnp.moveaxis(extra[s], (0, 1, 2), (2, 1, 0))[..., None] * out_x[s][None, :, None, :]
        for s in range(2)
    )
    all_y = exchange(
        state_y.reshape(2, lev, fields * cx).astype(jnp.bfloat16), ("gy",), 2, False
    ).astype(jnp.float32)
    ahead, behind, cross = combine_weights(
        filter_length, cy, lax.axis_size("gy"), lax.axis_index("gy")
    )
    enter_y = jnp.sum(ahead[:, :, None] * all_y[:, 0], axis=0)
    leave_y = jnp.sum(
        behind[:, :, None] * all_y[:, 1] + cross[:, :, None] * all_y[:, 0], axis=0
    )
    edges_y = left_terms(jnp.stack([enter_y, leave_y], axis=1))
    edges_x = right_terms(jnp.moveaxis(edges_x.reshape(2 * fields, lev, cy), 0, 1))
    depth_x, depth_y = block_x.shape[1], edges_y.shape[1]
    grad_alpha, static, *strips = pl.pallas_call(
        functools.partial(final_kernel, members),
        grid=(steps,),
        in_specs=[
            levels_first(fields * cx, cy),
            levels_first(depth_x, fields * cx),
            levels_first(depth_x, cy),
            levels_first(cy, cy),
            levels_first(depth_y, cy),
            levels_first(depth_y, fields * cx),
            levels_first(cx, cy),
            levels_first(cx, cy),
        ],
        out_specs=[
            pl.BlockSpec((members, tile, cx, cy), lambda i: (0, i, 0, 0)),
            levels_first(cx, cy),
            pl.BlockSpec((3, tile, STRIP, cy), lambda i: (0, i, 0, 0)),
            pl.BlockSpec((3, tile, STRIP, cy), lambda i: (0, i, 0, 0)),
            pl.BlockSpec((3, tile, STRIP, cx), lambda i: (0, i, 0, 0)),
            pl.BlockSpec((3, tile, STRIP, cx), lambda i: (0, i, 0, 0)),
        ],
        out_shape=[
            jax.ShapeDtypeStruct((members, lev, cx, cy), jnp.float32),
            jax.ShapeDtypeStruct((lev, cx, cy), jnp.float32),
            jax.ShapeDtypeStruct((3, lev, STRIP, cy), jnp.bfloat16),
            jax.ShapeDtypeStruct((3, lev, STRIP, cy), jnp.bfloat16),
            jax.ShapeDtypeStruct((3, lev, STRIP, cx), jnp.bfloat16),
            jax.ShapeDtypeStruct((3, lev, STRIP, cx), jnp.bfloat16),
        ],
        compiler_params=params,
        name="final",
    )(local, block_x, edges_x, smooth_y, out_y, edges_y, wind_u, wind_v)

    halo_x, halo_y = halo(*strips, 5)
    static = pl.pallas_call(
        transport_kernel,
        grid=(steps,),
        in_specs=[
            levels_first(cx, cy),
            levels_first(cx, cy),
            levels_first(cx, cy),
            pl.BlockSpec((2, 3, tile, STRIP, cy), lambda i: (0, 0, i, 0, 0)),
            pl.BlockSpec((3, 2, 3, tile, STRIP, cx), lambda i: (0, 0, 0, i, 0, 0)),
        ],
        out_specs=levels_first(cx, cy),
        out_shape=jax.ShapeDtypeStruct((lev, cx, cy), jnp.float32),
        compiler_params=params,
        name="transport",
    )(static, wind_u, wind_v, halo_x, halo_y)
    return (grad_alpha, static)


def solution(mesh):
    return jax.shard_map(
        body,
        mesh=mesh,
        in_specs=(
            P(None, "gx", "gy"),
            P(None, None, "gx", "gy"),
            P(None, "gx", "gy"),
            P(None, "gx", "gy"),
            P(),
            P(("gx", "gy"), None, None),
            P(("gx", "gy"), None),
            P(("gx", "gy"), None, None),
            P(("gx", "gy")),
            P(("gx", "gy")),
            P(("gx", "gy")),
        ),
        out_specs=(P(None, None, "gx", "gy"), P(None, "gx", "gy")),
        check_vma=False,
    )
```

profile of v0, /device:TPU:0, one launch (start us, length us, event | category | flops | bytes accessed | tf_op | source)
XLA Modules:
  0.0 193.6 jit_solution(7672344367806161307)
XLA Ops:
  0.7 0.9 convert_reduce_fusion
  1.6 0.7 multiply_add_fusion
  2.3 0.1 pad.60.clone
  2.4 0.7 exponential-minus-one_negate_fusion
  3.2 1.4 select_reduce_fusion
  4.8 0.1 negate_convert_fusion.1
  4.9 0.7 rsqrt_multiply_fusion
  5.5 0.9 fusion.47
  6.4 0.1 exponential_select_fusion.9
  6.5 0.1 multiply_reduce_fusion.10
  6.6 0.1 fusion.56
  6.7 0.1 slice_reduce_fusion
  6.8 0.1 negate_convert_fusion
  6.9 0.2 broadcast_select_fusion.9
  7.1 0.1 exponential_select_fusion.8
  7.2 0.1 multiply_reduce_fusion.2
  7.3 0.2 broadcast_select_fusion.8
  7.7 0.9 fusion.43
  8.9 1.0 divide_multiply_fusion
  9.8 0.1 reduce-precision_convert_fusion.4
  10.0 0.1 mul.1382
  10.1 0.8 fusion.50
  10.8 0.7 fusion.53
  11.7 0.1 copy.85
  11.8 0.1 copy.88
  11.9 0.8 copy.69
  12.6 0.9 fusion.32.uy_ref
  13.5 1.1 copy.102
  14.6 0.1 mul.1379
  14.7 0.4 copy.73
  15.1 0.4 fusion.10
  15.5 1.6 fusion.12.ux_ref
  17.1 41.4 %observe.1 = (s16[32,160,128]{2,1,0:T(8,128)(2,1)}, f32[32,1,128]{2,1,0:T(1,128)}) custom-call(s32[64]{0:T(128)} %get-tuple-element.40.order_ref, s32[64]{0:T(128)} %get-tuple-element.39.line_ref, s32[64]{0:T(128)} %get-tuple-element.38.count_ref, bf16[512,64]{1,0:T(8,128)(2,1)} %bitcast.174, f32[1,512]{1,0:T(1,128)} %w_ref.1, bf16[64,512,128]{2,1,0:T(8,128)(2,1)} %d_hbm.1), custom_call_target="tpu_custom_call" | custom-call | tf_op jit(solution)/shard_map/observe/pallas_call | solution.py:223
  58.5 0.9 fusion.8
  59.4 0.4 fusion.6
  59.9 2.6 %pad_maximum_fusion.mx_ref = bf16[64,56,144]{2,1,0:T(8,128)(2,1)} fusion(bf16[64,56,48]{2,1,0:T(8,128)(2,1)S(1)} %get-tuple-element.47, bf16[64,56,48]{2,1,0:T(8,128)(2,1)S(1)} %get-tuple-element.46), kind=kLoop, calls=%fused_computation.13 | loop fusion | flops 3096576 | bytes 1720320 | tf_op jit(solution)/shard_map/concatenate | solution.py:609
  62.5 2.3 %fusion.1.my_ref = f32[64,128,128]{2,1,0:T(8,128)S(1)} fusion(f32[128,128]{1,0:T(8,128)S(1)} %get-tuple-element.140, f32[64]{0:T(128)S(1)} %copy-done.4, f32[128,128]{1,0:T(8,128)S(1)} %get-tuple-element.141, f32[64]{0:T(128)S(1)} %get-tuple-element.43), kind=kLoop, calls=%fused_computation.2 | loop fusion | flops 5242880 | bytes 4325888 | tf_op jit(solution)/shard_map/mul | solution.py:510
  64.7 2.0 %copy-done = f32[64,128,128]{2,1,0:T(8,128)} copy-done((f32[64,128,128]{2,1,0:T(8,128)}, f32[64,128,128]{2,1,0:T(8,128)S(1)}, u32[]{:S(2)}) %copy-start) | copy-done | bytes 4194328
  66.8 0.1 pad_maximum_fusion.4
  66.9 1.2 fusion.23.wy_ref
  68.1 17.1 %local.1 = (f32[64,240,128]{2,1,0:T(8,128)}, bf16[10,64,128]{2,1,0:T(8,128)(2,1)}, f32[64,8,240]{2,1,0:T(8,128)}) custom-call(f32[32,1,128]{2,1,0:T(1,128)} %get-tuple-element.15.note_ref, s16[32,160,128]{2,1,0:T(8,128)(2,1)} %get-tuple-element.16.got_ref, bf16[48,64,128]{2,1,0:T(8,128)(2,1)} %bitcast.168, bf16[4,64,48,128]{3,2,1,0:T(8,128)(2,1)} %e_ref.1, ...), custom_call_target="tpu_custom_call" | custom-call | tf_op jit(solution)/shard_map/local/pallas_call | solution.py:642
  85.3 1.6 copy_bitcast_fusion.3.x_ref
  86.9 9.7 %exchange_1.1 = bf16[8,10,8,128]{3,2,1,0:T(8,128)(2,1)} custom-call(bf16[8,10,8,128]{3,2,1,0:T(8,128)(2,1)} %copy_bitcast_fusion.3.x_ref), custom_call_target="tpu_custom_call" | custom-call | tf_op jit(solution)/shard_map/exchange_1/pallas_call | solution.py:73
  96.6 0.9 convert_element_type.222
  97.6 0.3 add_convert_fusion
  97.8 0.2 add_convert_fusion.1
  98.0 0.7 pad_maximum_fusion.2.x_ref
  98.7 8.7 %exchange_4.1 = bf16[8,10,8,128]{3,2,1,0:T(8,128)(2,1)} custom-call(bf16[8,10,8,128]{3,2,1,0:T(8,128)(2,1)} %pad_maximum_fusion.2.x_ref), custom_call_target="tpu_custom_call" | custom-call | tf_op jit(solution)/shard_map/exchange_4/pallas_call | solution.py:73
  107.4 0.9 convert_bitcast_fusion
  108.4 0.3 multiply_reduce_fusion
  108.7 0.2 reduce-precision_convert_fusion.2
  109.0 1.1 fusion.25.ex_ref
  110.1 0.1 copy.89
  110.2 0.1 copy.86
  110.3 0.2 copy.82
  110.5 0.7 fusion.38.x_ref
  111.2 6.6 %exchange_2.1 = bf16[4,2,64,240]{3,2,1,0:T(8,128)(2,1)} custom-call(bf16[2,64,240]{2,1,0:T(8,128)(2,1)} %fusion.38.x_ref), custom_call_target="tpu_custom_call" | custom-call | tf_op jit(solution)/shard_map/exchange_2/pallas_call | solution.py:73
  117.8 1.0 convert_element_type.234
  118.8 0.2 multiply_reduce_fusion.1
  119.1 0.2 fusion.36
  119.2 1.1 fusion.27.ey_ref
  120.3 22.5 %final.1 = (f32[4,64,48,128]{3,2,1,0:T(8,128)}, f32[64,48,128]{2,1,0:T(8,128)}, bf16[3,64,4,128]{3,2,1,0:T(4,128)(2,1)}, bf16[3,64,4,128]{3,2,1,0:T(4,128)(2,1)}...) custom-call(f32[64,240,128]{2,1,0:T(8,128)} %get-tuple-element.17.x_ref, ...), custom_call_target="tpu_custom_call" | custom-call | tf_op jit(solution)/shard_map/final/pallas_call | solution.py:711
  142.8 24.5 %halo.1 = (bf16[2,3,64,4,128]{4,3,2,1,0:T(4,128)(2,1)}, bf16[3,2,3,64,4,48]{5,4,3,2,1,0:T(4,128)(2,1)}) custom-call(bf16[3,64,4,128]{3,2,1,0:T(4,128)(2,1)} %get-tuple-element.22.low_x, bf16[3,64,4,128]{3,2,1,0:T(4,128)(2,1)} %get-tuple-element.23.high_x, bf16[3,64,4,48]{3,2,1,0:T(4,128)(2,1)} %get-tuple-element.24.low_y, ...), custom_call_target="tpu_custom_call" | custom-call | tf_op jit(solution)/shard_map/halo/pallas_call | solution.py:358
  167.3 26.3 %transport.1 = f32[64,48,128]{2,1,0:T(8,128)} custom-call(f32[64,48,128]{2,1,0:T(8,128)} %get-tuple-element.21.s_ref, bf16[64,48,128]{2,1,0:T(8,128)(2,1)} %u_ref.3, bf16[64,48,128]{2,1,0:T(8,128)(2,1)} %v_ref.3, bf16[2,3,64,4,128]{4,3,2,1,0:T(4,128)(2,1)} %get-tuple-element.26.hx_ref, bf16[3,2,3,64,4,48]{5,4,3,2,1,0:T(4,128)(2,1)} %get-tuple-element.27.hy_ref), custom_call_target="tpu_custom_call" | custom-call | tf_op jit(solution)/shard_map/transport/pallas_call | solution.py:745
  (81 shorter events, 1.1 us)
Async XLA Ops:
  0.6 11.2 %copy-start.3 = (bf16[1,512,64]{1,2,0:T(8,128)(2,1)S(1)}, bf16[1,512,64]{1,2,0:T(8,128)(2,1)}, u32[]{:S(2)}) copy-start(bf16[1,512,64]{1,2,0:T(8,128)(2,1)} %param.16) | copy-start | bytes 196612
  0.6 12.9 %copy-start.1 = (bf16[64,48,128]{2,1,0:T(8,128)(2,1)S(1)}, bf16[64,48,128]{2,1,0:T(8,128)(2,1)}, u32[]{:S(2)}) copy-start(bf16[64,48,128]{2,1,0:T(8,128)(2,1)} %param.11) | copy-start | bytes 2359300
  17.1 41.4 %copy-start.4 = (f32[64]{0:T(128)S(1)}, f32[64]{0:T(128)}, u32[]{:S(2)}) copy-start(f32[64]{0:T(128)} %param.15) | copy-start | bytes 772
  64.7 2.0 %copy-start = (f32[64,128,128]{2,1,0:T(8,128)}, f32[64,128,128]{2,1,0:T(8,128)S(1)}, u32[]{:S(2)}) copy-start(f32[64,128,128]{2,1,0:T(8,128)S(1)} %fusion.1.my_ref) | copy-start | bytes 12582916
  108.4 1.9 copy-start.2
where the time goes:
time: 196 us; the launch traced here: 194 us
  Pallas kernels  157 us (80%)
  other arithmetic  28 us (14%)
  local copies, waits for them, and re-layouts  7.46 us (4%)
    pallas_call x1, Pallas kernels, observe(): pl.pallas_call(functools.partial(obs_kernel, axes, most), out_shape=[jax....  41.4 us
    pallas_call x1, Pallas kernels, body(): pl.pallas_call(transport_kernel, grid=(steps,), in_specs=[levels_first(cx...  26.3 us
    pallas_call x3, Pallas kernels, exchange(): pl.pallas_call(functools.partial(gather_kernel, axes, scatter), out_shape...  24.9 us
    pallas_call x1, Pallas kernels, halo(): pl.pallas_call(halo_kernel, out_shape=[jax.ShapeDtypeStruct((2,) + low_x....  24.5 us
    pallas_call x1, Pallas kernels, body(): pl.pallas_call(functools.partial(final_kernel, members), grid=(steps,), i...  22.5 us
    pallas_call x1, Pallas kernels, body(): pl.pallas_call(functools.partial(local_kernel, members, most), grid=(step...  17.1 us
    concatenate x4, other arithmetic, whole_tiles(): joined = jnp.concatenate(parts, axis=1)  4.59 us

commit v1 on v0

--- a/solution.py
+++ b/solution.py
@@ -18,73 +18,6 @@
         return {axes[0]: index}
     minor = lax.axis_size(axes[1])
     return {axes[0]: index // minor, axes[1]: index % minor}
-
-
-def gather_kernel(axes, scatter, x_ref, o_ref, send_sem, recv_sem, own_sem):
-    count = lax.axis_size(axes)
-    me = lax.axis_index(axes[0])
-    for name in axes[1:]:
-        me = me * lax.axis_size(name) + lax.axis_index(name)
-    barrier = pltpu.get_barrier_semaphore()
-
-    def greet(k, _):
-        pl.semaphore_signal(
-            barrier,
-            inc=1,
-            device_id=peer_id(axes, lax.rem(me + k, count)),
-            device_id_type=pl.DeviceIdType.MESH,
-        )
-        return 0
-
-    lax.fori_loop(1, count, greet, 0)
-    own = pltpu.make_async_copy(x_ref.at[me] if scatter else x_ref, o_ref.at[me], own_sem)
-    own.start()
-    pl.semaphore_wait(barrier, count - 1)
-
-    def copy(k, slot):
-        to = lax.rem(me + k, count)
-        return pltpu.make_async_remote_copy(
-            src_ref=x_ref.at[to] if scatter else x_ref,
-            dst_ref=o_ref.at[slot],
-            send_sem=send_sem.at[k],
-            recv_sem=recv_sem.at[k],
-            device_id=peer_id(axes, to),
-            device_id_type=pl.DeviceIdType.MESH,
-        )
-
-    def send(k, _):
-        copy(k, me).start()
-        return 0
-
-    def finish(k, _):
-        landed = copy(k, lax.rem(me + count - k, count))
-        landed.wait_send()
-        landed.wait_recv()
-        return 0
-
-    lax.fori_loop(1, count, send, 0)
-    own.wait()
-    lax.fori_loop(1, count, finish, 0)
-
-
-def exchange(x, axes, collective_id, scatter):
-    count = lax.axis_size(axes)
-    shape = x.shape if scatter else (count,) + x.shape
-    return pl.pallas_call(
-        functools.partial(gather_kernel, axes, scatter),
-        out_shape=jax.ShapeDtypeStruct(shape, x.dtype),
-        in_specs=[pl.BlockSpec(memory_space=pltpu.VMEM)],
-        out_specs=pl.BlockSpec(memory_space=pltpu.VMEM),
-        scratch_shapes=[
-            pltpu.SemaphoreType.DMA((count,)),
-            pltpu.SemaphoreType.DMA((count,)),
-            pltpu.SemaphoreType.DMA,
-        ],
-        compiler_params=pltpu.CompilerParams(
-            collective_id=collective_id, has_side_effects=True
-        ),
-        name="exchange_%d" % collective_id,
-    )(x)
 
 
 def split(value):
@@ -377,58 +310,149 @@
     return (col == jnp.where(row < width, row, row + cy - 2 * width)).astype(jnp.bfloat16)
 
 
-def local_kernel(
-    members, most, note_ref, got_ref, c_ref, e_ref, mx_ref, wy_ref,
-    x_ref, sx_ref, sy_ref, rows_ref, sum_ref,
+def fields_kernel(
+    members, most, note_ref, got_ref, c_ref, e_ref, coef_ref,
+    x_ref, state_ref, sum_ref, ens_ref, run_ref,
 ):
     _, levels, cx, cy = e_ref.shape
     lev = c_ref.shape[1]
+    fields = members + 1
+    pieces, _, part, _ = state_ref.shape
+    i = pl.program_id(0)
+
+    @pl.when(i == 0)
+    def _():
+        home_sums(most, note_ref, got_ref, c_ref, sum_ref)
+
+    for m in range(members):
+        for l in range(levels):
+            start = (m * levels + l) * cx
+            ens_ref[start : start + cx, :] = e_ref[m, l].astype(jnp.float32)
+    decay = jnp.exp(coef_ref[0])
+    scale = coef_ref[1]
+    state = [jnp.zeros((levels, cy), jnp.float32)] * fields
+    for x in range(cx):
+        base = sum_ref[pl.ds(x * lev + i * levels, levels), :] * scale
+        for k in range(fields):
+            value = base
+            if k:
+                value = base * ens_ref[pl.ds((k - 1) * levels * cx + x, levels, stride=cx), :]
+            state[k] = value + decay * state[k]
+            run_ref[k * cx + x] = state[k]
+    for j in range(pieces):
+        for k in range(fields):
+            state_ref[j, k] = state[k][j * part : (j + 1) * part].astype(state_ref.dtype)
+    state = [jnp.zeros((levels, cy), jnp.float32)] * fields
+    for x in reversed(range(cx)):
+        for k in range(fields):
+            state[k] = run_ref[k * cx + x] + decay * state[k]
+            x_ref[pl.ds(k * cx + x, levels, stride=fields * cx), :] = state[k]
+    for j in range(pieces):
+        for k in range(fields):
+            state_ref[j, fields + k] = state[k][j * part : (j + 1) * part].astype(state_ref.dtype)
+
+
+def carry_x_kernel(cells, s_ref, coef_ref, o_ref, in_ref, mid_ref, out_ref, sems):
+    size = lax.axis_size("gx")
+    me = lax.axis_index("gx")
+    fields = s_ref.shape[1] // 2
+    barrier = pltpu.get_barrier_semaphore()
+
+    def greet(k, _):
+        pl.semaphore_signal(
+            barrier,
+            inc=1,
+            device_id={"gx": lax.rem(me + k, size)},
+            device_id_type=pl.DeviceIdType.MESH,
+        )
+        return 0
+
+    lax.fori_loop(1, size, greet, 0)
+    in_ref[me] = s_ref[me]
+    pl.semaphore_wait(barrier, size - 1)
+
+    def copy(source, target, first, to, slot):
+        return pltpu.make_async_remote_copy(
+            src_ref=source.at[to],
+            dst_ref=target.at[slot],
+            send_sem=sems.at[first, to],
+            recv_sem=sems.at[first + 1, slot],
+            device_id={"gx": to},
+            device_id_type=pl.DeviceIdType.MESH,
+        )
+
+    def swap(source, target, first):
+        def send(k, _):
+            copy(source, target, first, lax.rem(me + k, size), me).start()
+            return 0
+
+        def finish(k, _):
+            peer = lax.rem(me + k, size)
+            landed = copy(source, target, first, peer, peer)
+            landed.wait_send()
+            landed.wait_recv()
+            return 0
+
+        lax.fori_loop(1, size, send, 0)
+        lax.fori_loop(1, size, finish, 0)
+
+    swap(s_ref, in_ref, 0)
+    rate = coef_ref[me, 0]
+    step = jnp.exp(rate * cells)
+    link = coef_ref[me, 2] * (jnp.exp(rate) - jnp.exp(rate * (2 * cells + 1)))
+    for k in range(fields):
+        enter = jnp.zeros(rate.shape, jnp.float32)
+        entered = []
+        for t in range(size):
+            entered.append(enter)
+            mid_ref[t, k] = enter.astype(mid_ref.dtype)
+            enter = in_ref[t, k].astype(jnp.float32) + step * enter
+        leave = jnp.zeros(rate.shape, jnp.float32)
+        for t in reversed(range(size)):
+            mid_ref[t, fields + k] = leave.astype(mid_ref.dtype)
+            leave = in_ref[t, fields + k].astype(jnp.float32) + link * entered[t] + step * leave
+    out_ref[me] = mid_ref[me]
+    swap(mid_ref, out_ref, 2)
+    parts, part = out_ref.shape[0], out_ref.shape[2]
+    for t in range(parts):
+        for k in range(2 * fields):
+            o_ref[k, t * part : (t + 1) * part, :] = out_ref[t, k].astype(jnp.float32)
+
+
+def rows_kernel(fields, x_ref, enter_ref, coef_ref, z_ref, state_ref, rows_ref, far_ref, sum_ref):
+    levels, _, cy = z_ref.shape
+    cx = z_ref.shape[1] // fields
+    along = lax.broadcasted_iota(jnp.int32, (cx, cy), 0).astype(jnp.float32)
 
     @pl.when(pl.program_id(0) == 0)
     def _():
-        home_sums(most, note_ref, got_ref, c_ref, sum_ref)
-
+        row = lax.broadcasted_iota(jnp.int32, (cy, cy), 0)
+        col = lax.broadcasted_iota(jnp.int32, (cy, cy), 1)
+        far_ref[...] = jnp.abs(row - col).astype(jnp.float32)
+        sum_ref[...] = (2 * cy - row - col).astype(jnp.float32)
+
+    row = lax.broadcasted_iota(jnp.int32, (8, cy), 0)
+    col = lax.broadcasted_iota(jnp.int32, (8, cy), 1)
+    picks = (col == jnp.where(row == 0, cy - 1, jnp.where(row == 1, 0, -1))).astype(jnp.bfloat16)
     for l in range(levels):
-        base = sum_ref[pl.ds(pl.program_id(0) * levels + l, cx, stride=lev), :]
-        parts = [base] + [e_ref[m, l].astype(jnp.float32) * base for m in range(members)]
-        high, low = split(jnp.concatenate(parts, axis=1))
-        result = jnp.dot(
-            mx_ref[l],
-            jnp.concatenate([high, high, low], axis=0),
-            preferred_element_type=jnp.float32,
-        )
-        stack = jnp.concatenate(
-            [result[:cx, m * cy : (m + 1) * cy] for m in range(members + 1)], axis=0
-        )
-        x_ref[l] = stack
-        for m in range(members + 1):
-            rows_ref[m, l : l + 1, :] = result[cx : cx + 1, m * cy : (m + 1) * cy]
-            rows_ref[members + 1 + m, l : l + 1, :] = result[0:1, m * cy : (m + 1) * cy]
-        high, low = split(stack)
-        sums = lax.dot_general(
-            wy_ref[l],
-            jnp.concatenate([high, low], axis=1),
-            (((1,), (1,)), ((), ())),
-            preferred_element_type=jnp.float32,
-        )
-        sy_ref[l] = sums[0:8] + sums[8:16]
-    sx_ref[...] = rows_ref[...].astype(sx_ref.dtype)
-
-
-def final_kernel(
-    members, x_ref, ux_ref, ex_ref, my_ref, uy_ref, ey_ref, u_ref, v_ref,
-    a_ref, s_ref, low_x, high_x, low_y, high_y,
-):
-    levels = x_ref.shape[0]
-    _, _, cx, cy = a_ref.shape
-    first = (((0,), (0,)), ((), ()))
-    columns = edge_columns(cy, STRIP)
-    for l in range(levels):
-        field = x_ref[l] + lax.dot_general(
-            ux_ref[l], ex_ref[l], first, preferred_element_type=jnp.float32
-        )
-        high, low = split(field)
-        m_high, m_low = split(my_ref[l])
+        rate = coef_ref[0, l : l + 1, :]
+        tall = coef_ref[2, l : l + 1, :]
+        ahead = tall * (jnp.exp((along + 1.0) * rate) - jnp.exp((2.0 * cx + 1.0 - along) * rate))
+        behind = jnp.exp((cx - along) * rate)
+        parts = []
+        for k in range(fields):
+            parts.append(
+                x_ref[l, k * cx : (k + 1) * cx, :]
+                + ahead * enter_ref[k, l : l + 1, :]
+                + behind * enter_ref[fields + k, l : l + 1, :]
+            )
+        high, low = split(jnp.concatenate(parts, axis=0))
+        smooth = (
+            coef_ref[1, l : l + 1, :]
+            * tall
+            * (jnp.exp(far_ref[...] * rate) - jnp.exp(sum_ref[...] * rate))
+        )
+        m_high, m_low = split(smooth)
         weights = jnp.concatenate(
             [
                 jnp.concatenate([m_high, m_low], axis=1),
@@ -439,10 +463,100 @@
         both = jnp.dot(
             jnp.concatenate([high, low], axis=1), weights, preferred_element_type=jnp.float32
         )
-        field = (
-            both[:, :cy]
-            + both[:, cy:]
-            + lax.dot_general(ey_ref[l], uy_ref[l], first, preferred_element_type=jnp.float32)
+        z = both[:, :cy] + both[:, cy:]
+        z_ref[l] = z
+        ends = lax.dot_general(
+            picks,
+            z.astype(jnp.bfloat16),
+            (((1,), (1,)), ((), ())),
+            preferred_element_type=jnp.float32,
+        )
+        rows_ref[0, l : l + 1, :] = ends[0:1]
+        rows_ref[1, l : l + 1, :] = ends[1:2]
+    state_ref[...] = rows_ref[...].astype(state_ref.dtype)
+
+
+def carry_y_kernel(cells, s_ref, coef_ref, o_ref, in_ref, sems):
+    size = lax.axis_size("gy")
+    me = lax.axis_index("gy")
+    _, lev, width = s_ref.shape
+    barrier = pltpu.get_barrier_semaphore()
+    for k in range(1, size):
+        pl.semaphore_signal(
+            barrier,
+            inc=1,
+            device_id={"gy": lax.rem(me + k, size)},
+            device_id_type=pl.DeviceIdType.MESH,
+        )
+    in_ref[me] = s_ref[...]
+    pl.semaphore_wait(barrier, size - 1)
+
+    def copy(to, slot):
+        return pltpu.make_async_remote_copy(
+            src_ref=s_ref,
+            dst_ref=in_ref.at[slot],
+            send_sem=sems.at[0, to],
+            recv_sem=sems.at[1, slot],
+            device_id={"gy": to},
+            device_id_type=pl.DeviceIdType.MESH,
+        )
+
+    for k in range(1, size):
+        copy(lax.rem(me + k, size), me).start()
+    for k in range(1, size):
+        peer = lax.rem(me + k, size)
+        landed = copy(peer, peer)
+        landed.wait_send()
+        landed.wait_recv()
+    rate = coef_ref[0, :, 0:1]
+    step = jnp.broadcast_to(jnp.exp(rate * cells), (lev, width))
+    link = coef_ref[2, :, 0:1] * (jnp.exp(rate) - jnp.exp(rate * (2 * cells + 1)))
+    link = jnp.broadcast_to(link, (lev, width))
+    enter = jnp.zeros((lev, width), jnp.float32)
+    mine = enter
+    entered = []
+    for t in range(size):
+        entered.append(enter)
+        mine = jnp.where(me == t, enter, mine)
+        enter = in_ref[t, 0].astype(jnp.float32) + step * enter
+    leave = jnp.zeros((lev, width), jnp.float32)
+    last = leave
+    for t in reversed(range(size)):
+        last = jnp.where(me == t, leave, last)
+        leave = in_ref[t, 1].astype(jnp.float32) + link * entered[t] + step * leave
+    o_ref[0] = mine
+    o_ref[1] = last
+
+
+def ends_of(first, second):
+    row = lax.broadcasted_iota(jnp.int32, (8, first.shape[1]), 0)
+    parts = [jnp.broadcast_to(v, row.shape) for v in (first, second)]
+    (a, b), (c, d) = [[p.astype(jnp.float32) for p in split(v)] for v in parts]
+    return row, a, b, c, d
+
+
+def final_kernel(
+    members, z_ref, y_ref, coef_ref, u_ref, v_ref,
+    a_ref, s_ref, low_x, high_x, low_y, high_y,
+):
+    _, levels, cx, cy = a_ref.shape
+    columns = edge_columns(cy, STRIP)
+    along = lax.broadcasted_iota(jnp.int32, (1, cy), 1).astype(jnp.float32)
+    for l in range(levels):
+        rate = coef_ref[0, l : l + 1, :]
+        tall = coef_ref[2, l : l + 1, :]
+        ahead = tall * (jnp.exp((along + 1.0) * rate) - jnp.exp((2.0 * cy + 1.0 - along) * rate))
+        behind = jnp.exp((cy - along) * rate)
+        row, a, b, c, d = ends_of(ahead, behind)
+        across = jnp.where(row < 2, a, jnp.where(row == 2, b, jnp.where(row < 5, c, d)))
+        row, a, b, c, d = ends_of(y_ref[0, l : l + 1, :], y_ref[1, l : l + 1, :])
+        down = jnp.where(row % 3 == 1, jnp.where(row < 3, b, d), jnp.where(row < 3, a, c))
+        down = jnp.where(row < 6, down, 0.0)
+        field = z_ref[l] + lax.dot_general(
+            down.astype(jnp.bfloat16),
+            across.astype(jnp.bfloat16),
+            (((0,), (0,)), ((), ())),
+            preferred_element_type=jnp.float32,
         )
         static = field[:cx]
         s_ref[l] = static
@@ -499,69 +613,6 @@
             s = s + u * (jnp.where(east, pltpu.roll(s, 1, 0), pltpu.roll(s, rows - 1, 0)) - s)
             s = s + v * (jnp.where(north, pltpu.roll(s, 1, 1), pltpu.roll(s, lanes - 1, 1)) - s)
         o_ref[l] = s[EDGE : EDGE + cx, :cy]
-
-
-def smoother(lengths, count):
-    pos = jnp.arange(count, dtype=jnp.float32)
-    far = jnp.abs(pos[:, None] - pos[None, :])
-    left = count - jnp.maximum(pos[:, None], pos[None, :])
-    lengths = lengths[:, None, None]
-    scale = -jnp.expm1(-1.0 / lengths) / jnp.sqrt(-jnp.expm1(-2.0 / lengths))
-    return scale * jnp.exp(-far[None] / lengths) * -jnp.expm1(-2.0 * left[None] / lengths)
-
-
-def end_weights(lengths, count):
-    pos = jnp.arange(count, dtype=jnp.float32)
-    coef = jnp.sqrt(-jnp.expm1(-2.0 / lengths))
-    return coef[:, None] * jnp.exp(-(count - 1.0 - pos)[None, :] / lengths[:, None])
-
-
-def responses(lengths, count):
-    pos = jnp.arange(count, dtype=jnp.float32)[None, :]
-    lengths = lengths[:, None]
-    coef = -jnp.expm1(-1.0 / lengths)
-    ratio = jnp.expm1(-2.0 * (count - pos) / lengths) / jnp.expm1(-2.0 / lengths)
-    ahead = coef * jnp.exp(-(pos + 1.0) / lengths) * ratio
-    behind = jnp.exp(-(count - pos) / lengths)
-    return ahead, behind
-
-
-def combine_weights(lengths, count, size, me):
-    link = responses(lengths, count)[0][:, 0]
-    k = jnp.arange(size)
-
-    def power(steps, ok):
-        return jnp.where(
-            ok[..., None],
-            jnp.exp(-jnp.maximum(steps, 0)[..., None] * (count / lengths)),
-            0.0,
-        )
-
-    ahead = power(me - 1 - k, k < me)
-    behind = power(k - me - 1, k > me)
-    pair = power(k[:, None] - 1 - k[None, :], k[None, :] < k[:, None])
-    cross = link[None, :] * jnp.sum(behind[:, None, :] * pair, axis=0)
-    return ahead, behind, cross
-
-
-def two_parts(value):
-    high = lax.reduce_precision(value, 8, 7)
-    return high, value - high
-
-
-def whole_tiles(parts):
-    joined = jnp.concatenate(parts, axis=1)
-    return jnp.pad(joined, ((0, 0), (0, -joined.shape[1] % 16), (0, 0))).astype(jnp.bfloat16)
-
-
-def left_terms(value):
-    high, low = two_parts(value)
-    return whole_tiles([high, low, high])
-
-
-def right_terms(value):
-    high, low = two_parts(value)
-    return whole_tiles([high, high, low])
 
 
 def body(
@@ -596,138 +647,122 @@
     got, note = observe(
         order, lines, counts, jacobian[0], obs_weight, departure, axes, most, 3
     )
-    smooth_x = smoother(filter_length, cx)
-    rows_x = jnp.concatenate(
-        [
-            smooth_x,
-            end_weights(filter_length, cx)[:, None, :],
-            jnp.zeros((lev, EDGE - 1, cx), jnp.float32),
-        ],
-        axis=1,
-    )
-    high_x = lax.reduce_precision(rows_x, 8, 7)
-    cat_x = jnp.concatenate([high_x, rows_x - high_x, high_x], axis=2).astype(jnp.bfloat16)
-    smooth_y = smoother(filter_length, cy)
-    sums_y = jnp.stack([end_weights(filter_length, cy), smooth_y[:, 0, :]], axis=1)
-    high_y = lax.reduce_precision(sums_y, 8, 7)
-    low_y = sums_y - high_y
-    blank = jnp.zeros((lev, 6, 2 * cy), jnp.float32)
-    cat_y = jnp.concatenate(
-        [
-            jnp.concatenate([high_y, high_y], axis=2),
-            blank,
-            jnp.concatenate([low_y, jnp.zeros_like(low_y)], axis=2),
-            blank,
-        ],
-        axis=1,
-    ).astype(jnp.bfloat16)
-
-    out_x = jnp.stack(responses(filter_length, cx), axis=0)
-    same = jnp.eye(fields, dtype=jnp.float32)
-    block_x = left_terms(
-        (
-            jnp.moveaxis(out_x, 0, 1)[:, :, None, None, :] * same[None, None, :, :, None]
-        ).reshape(lev, 2 * fields, fields * cx)
-    )
-    out_y = right_terms(jnp.stack(responses(filter_length, cy), axis=1))
     across = jnp.transpose(increment, (1, 0, 2))
-    tile = 16
+    rate = -1.0 / filter_length
+    tall = -1.0 / jnp.expm1(2.0 * rate)
+    gain = -jnp.expm1(rate) * jnp.sqrt(-jnp.expm1(2.0 * rate))
+    coef = jnp.broadcast_to(jnp.stack([rate, gain, tall])[:, :, None], (3, lev, cy))
+    size_x, size_y = lax.axis_size("gx"), lax.axis_size("gy")
+    part = lev // size_x
+    tile = 8
     steps = lev // tile
+    pieces = tile // part
+
     def levels_first(*shape):
         return pl.BlockSpec((tile,) + shape, lambda i: (i, 0, 0))
+
+    def levels_second(*shape):
+        first, *rest = shape
+        return pl.BlockSpec((first, tile) + tuple(rest), lambda i: (0, i) + (0,) * len(rest))
+
+    def whole(array):
+        return pl.BlockSpec(
+            array.shape, lambda i: (0,) * array.ndim, pipeline_mode=pl.Buffered(1)
+        )
 
     params = pltpu.CompilerParams(
         dimension_semantics=("arbitrary",), vmem_limit_bytes=56 * 1024 * 1024
     )
-    local, state_x, state_y = pl.pallas_call(
-        functools.partial(local_kernel, members, most),
+    rows = fields * cx
+    local, state_x = pl.pallas_call(
+        functools.partial(fields_kernel, members, most),
         grid=(steps,),
         in_specs=[
             pl.BlockSpec(memory_space=pltpu.SMEM),
-            pl.BlockSpec(got.shape, lambda i: (0, 0, 0), pipeline_mode=pl.Buffered(1)),
-            pl.BlockSpec(across.shape, lambda i: (0, 0, 0), pipeline_mode=pl.Buffered(1)),
-            pl.BlockSpec((members, tile, cx, cy), lambda i: (0, i, 0, 0)),
-            levels_first(cx + EDGE, 3 * cx),
-            levels_first(16, 2 * cy),
+            whole(got),
+            whole(across),
+            levels_second(members, cx, cy),
+            levels_second(3, cy),
         ],
         out_specs=[
-            levels_first(fields * cx, cy),
-            pl.BlockSpec((2 * fields, tile, cy), lambda i: (0, i, 0)),
-            levels_first(8, fields * cx),
+            pl.BlockSpec((tile * rows, cy), lambda i: (i, 0)),
+            pl.BlockSpec((pieces, 2 * fields, part, cy), lambda i: (i, 0, 0, 0)),
         ],
         out_shape=[
-            jax.ShapeDtypeStruct((lev, fields * cx, cy), jnp.float32),
-            jax.ShapeDtypeStruct((2 * fields, lev, cy), jnp.bfloat16),
-            jax.ShapeDtypeStruct((lev, 8, fields * cx), jnp.float32),
+            jax.ShapeDtypeStruct((lev * rows, cy), jnp.float32),
+            jax.ShapeDtypeStruct((size_x, 2 * fields, part, cy), jnp.bfloat16),
         ],
         scratch_shapes=[
-            pltpu.VMEM((2 * fields, tile, cy), jnp.float32),
             pltpu.VMEM((cx * lev, cy), jnp.float32),
+            pltpu.VMEM((members * tile * cx, cy), jnp.float32),
+            pltpu.VMEM((rows, tile, cy), jnp.float32),
         ],
         compiler_params=params,
-        name="local",
-    )(note, got, across, ensemble, cat_x, cat_y)
-
-    size_x = lax.axis_size("gx")
-    part = lev // size_x
-    own = lax.axis_index("gx") * part
-    mine = lax.dynamic_slice_in_dim(filter_length, own, part, 0)
-    sent = jnp.moveaxis(state_x.reshape(2 * fields, size_x, part, cy), 1, 0)
-    all_x = exchange(sent, ("gx",), 1, True).astype(jnp.float32)
-    ahead, behind, cross = [
-        jnp.stack(w) for w in zip(*[combine_weights(mine, cx, size_x, d) for d in range(size_x)])
-    ]
-    front, back = all_x[:, :fields], all_x[:, fields:]
-    enter_x = sum(ahead[:, k, None, :, None] * front[k][None] for k in range(size_x))
-    leave_x = sum(
-        behind[:, k, None, :, None] * back[k][None] + cross[:, k, None, :, None] * front[k][None]
-        for k in range(size_x)
-    )
-    swept = jnp.concatenate([enter_x, leave_x], axis=1).astype(jnp.bfloat16)
-    swept = exchange(swept, ("gx",), 4, True).astype(jnp.float32)
-    swept = jnp.moveaxis(swept, 0, 1).reshape(2, fields, lev, cy)
-    enter_x, leave_x = swept[0], swept[1]
-    edges_x = jnp.stack([enter_x, leave_x], axis=0)
-    extra = jnp.sum(
-        edges_x[:, :, :, None, :] * jnp.moveaxis(sums_y, 1, 1)[None, None], axis=-1
-    )
-    state_y = jnp.moveaxis(state_y[:, :2], 1, 0).reshape(2, lev, fields, cx) + sum(
-        jnp.moveaxis(extra[s], (0, 1, 2), (2, 1, 0))[..., None] * out_x[s][None, :, None, :]
-        for s in range(2)
-    )
-    all_y = exchange(
-        state_y.reshape(2, lev, fields * cx).astype(jnp.bfloat16), ("gy",), 2, False
-    ).astype(jnp.float32)
-    ahead, behind, cross = combine_weights(
-        filter_length, cy, lax.axis_size("gy"), lax.axis_index("gy")
-    )
-    enter_y = jnp.sum(ahead[:, :, None] * all_y[:, 0], axis=0)
-    leave_y = jnp.sum(
-        behind[:, :, None] * all_y[:, 1] + cross[:, :, None] * all_y[:, 0], axis=0
-    )
-    edges_y = left_terms(jnp.stack([enter_y, leave_y], axis=1))
-    edges_x = right_terms(jnp.moveaxis(edges_x.reshape(2 * fields, lev, cy), 0, 1))
-    depth_x, depth_y = block_x.shape[1], edges_y.shape[1]
+        name="fields",
+    )(note, got, across, ensemble, coef)
+    local = local.reshape(lev, rows, cy)
+
+    vmem = pl.BlockSpec(memory_space=pltpu.VMEM)
+    split_coef = jnp.moveaxis(coef.reshape(3, size_x, part, cy), 1, 0)
+    swept = pl.pallas_call(
+        functools.partial(carry_x_kernel, cx),
+        out_shape=jax.ShapeDtypeStruct((2 * fields, lev, cy), jnp.float32),
+        in_specs=[vmem, vmem],
+        out_specs=vmem,
+        scratch_shapes=[pltpu.VMEM(state_x.shape, jnp.bfloat16)] * 3
+        + [pltpu.SemaphoreType.DMA((4, size_x))],
+        compiler_params=pltpu.CompilerParams(collective_id=1, has_side_effects=True),
+        name="carry_x",
+    )(state_x, split_coef)
+
+    z, state_y = pl.pallas_call(
+        functools.partial(rows_kernel, fields),
+        grid=(steps,),
+        in_specs=[levels_first(rows, cy), levels_second(2 * fields, cy), levels_second(3, cy)],
+        out_specs=[levels_first(rows, cy), levels_second(2, rows)],
+        out_shape=[
+            jax.ShapeDtypeStruct((lev, rows, cy), jnp.float32),
+            jax.ShapeDtypeStruct((2, lev, rows), jnp.bfloat16),
+        ],
+        scratch_shapes=[
+            pltpu.VMEM((2, tile, rows), jnp.float32),
+            pltpu.VMEM((cy, cy), jnp.float32),
+            pltpu.VMEM((cy, cy), jnp.float32),
+        ],
+        compiler_params=params,
+        name="rows",
+    )(local, swept, coef)
+
+    entered = pl.pallas_call(
+        functools.partial(carry_y_kernel, cy),
+        out_shape=jax.ShapeDtypeStruct((2, lev, rows), jnp.float32),
+        in_specs=[vmem, vmem],
+        out_specs=vmem,
+        scratch_shapes=[
+            pltpu.VMEM((size_y, 2, lev, rows), jnp.bfloat16),
+            pltpu.SemaphoreType.DMA((2, size_y)),
+        ],
+        compiler_params=pltpu.CompilerParams(collective_id=2, has_side_effects=True),
+        name="carry_y",
+    )(state_y, coef)
+
     grad_alpha, static, *strips = pl.pallas_call(
         functools.partial(final_kernel, members),
         grid=(steps,),
         in_specs=[
-            levels_first(fields * cx, cy),
-            levels_first(depth_x, fields * cx),
-            levels_first(depth_x, cy),
-            levels_first(cy, cy),
-            levels_first(depth_y, cy),
-            levels_first(depth_y, fields * cx),
+            levels_first(rows, cy),
+            levels_second(2, rows),
+            levels_second(3, cy),
             levels_first(cx, cy),
             levels_first(cx, cy),
         ],
         out_specs=[
-            pl.BlockSpec((members, tile, cx, cy), lambda i: (0, i, 0, 0)),
+            levels_second(members, cx, cy),
             levels_first(cx, cy),
-            pl.BlockSpec((3, tile, STRIP, cy), lambda i: (0, i, 0, 0)),
-            pl.BlockSpec((3, tile, STRIP, cy), lambda i: (0, i, 0, 0)),
-            pl.BlockSpec((3, tile, STRIP, cx), lambda i: (0, i, 0, 0)),
-            pl.BlockSpec((3, tile, STRIP, cx), lambda i: (0, i, 0, 0)),
+            levels_second(3, STRIP, cy),
+            levels_second(3, STRIP, cy),
+            levels_second(3, STRIP, cx),
+            levels_second(3, STRIP, cx),
         ],
         out_shape=[
             jax.ShapeDtypeStruct((members, lev, cx, cy), jnp.float32),
@@ -739,7 +774,7 @@
         ],
         compiler_params=params,
         name="final",
-    )(local, block_x, edges_x, smooth_y, out_y, edges_y, wind_u, wind_v)
+    )(z, entered, coef, wind_u, wind_v)
 
     halo_x, halo_y = halo(*strips, 5)
     static = pl.pallas_call(

time: 196 us -> 162 us (0.83)
  other arithmetic: 28 us -> 3.65 us
  Pallas kernels: 157 us -> 149 us
  local copies, waits for them, and re-layouts: 7.46 us -> 5.5 us
    concatenate x7 -> x0, other arithmetic: 9.08 us -> none  [the longest x4 4.59 us: whole_tiles(): joined = jnp.concatenate(parts, axis=1)]
    pallas_call x4, Pallas kernels: 42.1 us -> 50 us  [the longest x1 16.9 us: body(): pl.pallas_call(functools.partial(fields_kernel, members, most), grid=(ste...]
    pallas_call x1, Pallas kernels: 22.5 us -> 14.8 us  [body(): pl.pallas_call(functools.partial(final_kernel, members), grid=(steps,), i...]
    pallas_call x1, Pallas kernels: 26.3 us -> 19.4 us  [body(): pl.pallas_call(transport_kernel, grid=(steps,), in_specs=[levels_first(cx...]
    mul x12 -> x1, other arithmetic: 6.66 us -> 0.67 us  [body(): gain = -jnp.expm1(rate) * jnp.sqrt(-jnp.expm1(2.0 * rate))]
    convert_element_type x15 -> x0, other arithmetic: 2.8 us -> none  [the longest x1 0.99 us: body(): all_y = exchange(state_y.reshape(2, lev, fields * cx).astype(jnp.bfloat16...]
where the time goes in v1:
time: 162 us; the launch traced here: 159 us
  Pallas kernels  149 us (92%)
  local copies, waits for them, and re-layouts  5.5 us (3%)
  other arithmetic  3.65 us (2%)
    pallas_call x1, Pallas kernels, observe(): pl.pallas_call(functools.partial(obs_kernel, axes, most), out_shape=[jax....  41.2 us
    pallas_call x1, Pallas kernels, halo(): pl.pallas_call(halo_kernel, out_shape=[jax.ShapeDtypeStruct((2,) + low_x....  23.5 us
    pallas_call x1, Pallas kernels, body(): pl.pallas_call(transport_kernel, grid=(steps,), in_specs=[levels_first(cx...  19.4 us
    pallas_call x1, Pallas kernels, body(): pl.pallas_call(functools.partial(fields_kernel, members, most), grid=(ste...  16.9 us
    pallas_call x1, Pallas kernels, body(): pl.pallas_call(functools.partial(carry_x_kernel, cx), out_shape=jax.Shape...  15.5 us
    pallas_call x1, Pallas kernels, body(): pl.pallas_call(functools.partial(final_kernel, members), grid=(steps,), i...  14.8 us
    pallas_call x1, Pallas kernels, body(): pl.pallas_call(functools.partial(rows_kernel, fields), grid=(steps,), in_...  10.8 us
    pallas_call x1, Pallas kernels, body(): pl.pallas_call(functools.partial(carry_y_kernel, cy), out_shape=jax.Shape...  6.75 us

profile of v1, /device:TPU:0, one launch (start us, length us, event | category | flops | bytes accessed | tf_op | source)
XLA Modules:
  0.0 158.8 jit_solution(10069385420924963996)
XLA Ops:
  0.6 0.9 convert_reduce_fusion
  1.5 0.7 multiply_add_fusion
  2.2 1.4 select_reduce_fusion
  3.6 0.7 sqrt_multiply_fusion
  4.3 0.1 stack.26
  4.4 0.1 stack.25
  4.5 0.1 stack.24
  4.6 0.7 broadcast_bitcast_fusion.coef_ref
  5.3 0.7 broadcast_in_dim.42.coef_ref
  6.0 1.6 %copy.16 = bf16[1,512,64]{2,1,0:T(8,128)(2,1)} copy(bf16[1,512,64]{1,2,0:T(8,128)(2,1)} %param.16) | data formatting | bytes 131072 | tf_op args[5]
  7.6 2.2 %copy.20 = bf16[64,48,128]{2,0,1:T(8,128)(2,1)} copy(bf16[64,48,128]{2,1,0:T(8,128)(2,1)} %param.11) | data formatting | bytes 1572864 | tf_op args[0]
  9.8 41.2 %observe.1 = (s16[32,160,128]{2,1,0:T(8,128)(2,1)}, f32[32,1,128]{2,1,0:T(1,128)}) custom-call(s32[64]{0:T(128)} %get-tuple-element.32.order_ref, s32[64]{0:T(128)} %get-tuple-element.31.line_ref, s32[64]{0:T(128)} %get-tuple-element.30.count_ref, bf16[512,64]{1,0:T(8,128)(2,1)} %bitcast.13, f32[1,512]{1,0:T(1,128)} %w_ref.1, bf16[64,512,128]{2,1,0:T(8,128)(2,1)} %d_hbm.1), custom_call_target="tpu_custom_call" | custom-call | tf_op jit(solution)/shard_map/observe/pallas_call | solution.py:156
  51.1 16.9 %fields.1 = (f32[15360,128]{1,0:T(8,128)}, bf16[8,10,8,128]{3,2,1,0:T(8,128)(2,1)}) custom-call(f32[32,1,128]{2,1,0:T(1,128)} %get-tuple-element.16.note_ref, s16[32,160,128]{2,1,0:T(8,128)(2,1)} %get-tuple-element.17.got_ref, bf16[48,64,128]{2,1,0:T(8,128)(2,1)} %bitcast.12, bf16[4,64,48,128]{3,2,1,0:T(8,128)(2,1)} %e_ref.1, ...), custom_call_target="tpu_custom_call" | custom-call | tf_op jit(solution)/shard_map/fields/pallas_call | solution.py:677
  67.9 15.5 %carry_x.1.enter_ref = f32[10,64,128]{2,1,0:T(8,128)} custom-call(bf16[8,10,8,128]{3,2,1,0:T(8,128)(2,1)} %get-tuple-element.19.s_ref, f32[8,3,8,128]{3,2,1,0:T(8,128)} %broadcast_bitcast_fusion.coef_ref), custom_call_target="tpu_custom_call" | custom-call | tf_op jit(solution)/shard_map/carry_x/pallas_call | solution.py:707
  83.4 10.8 %rows.1 = (f32[64,240,128]{2,1,0:T(8,128)}, bf16[2,64,240]{2,1,0:T(8,128)(2,1)}) custom-call(f32[64,240,128]{2,1,0:T(8,128)} %bitcast.11, f32[10,64,128]{2,1,0:T(8,128)} %carry_x.1.enter_ref, f32[3,64,128]{2,1,0:T(8,128)} %broadcast_in_dim.42.coef_ref), custom_call_target="tpu_custom_call" | custom-call | tf_op jit(solution)/shard_map/rows/pallas_call | solution.py:718
  94.3 6.8 %carry_y.1.y_ref = f32[2,64,240]{2,1,0:T(8,128)} custom-call(bf16[2,64,240]{2,1,0:T(8,128)(2,1)} %get-tuple-element.21.s_ref, f32[3,64,128]{2,1,0:T(8,128)} %broadcast_in_dim.42.coef_ref), custom_call_target="tpu_custom_call" | custom-call | tf_op jit(solution)/shard_map/carry_y/pallas_call | solution.py:736
  101.0 14.8 %final.1 = (f32[4,64,48,128]{3,2,1,0:T(8,128)}, f32[64,48,128]{2,1,0:T(8,128)}, bf16[3,64,4,128]{3,2,1,0:T(4,128)(2,1)}, bf16[3,64,4,128]{3,2,1,0:T(4,128)(2,1)}...) custom-call(f32[64,240,128]{2,1,0:T(8,128)} %get-tuple-element.20.z_ref, f32[2,64,240]{2,1,0:T(8,128)} %carry_y.1.y_ref, ...), custom_call_target="tpu_custom_call" | custom-call | tf_op jit(solution)/shard_map/final/pallas_call | solution.py:749
  115.9 23.5 %halo.1 = (bf16[2,3,64,4,128]{4,3,2,1,0:T(4,128)(2,1)}, bf16[3,2,3,64,4,48]{5,4,3,2,1,0:T(4,128)(2,1)}) custom-call(bf16[3,64,4,128]{3,2,1,0:T(4,128)(2,1)} %get-tuple-element.24.low_x, bf16[3,64,4,128]{3,2,1,0:T(4,128)(2,1)} %get-tuple-element.25.high_x, bf16[3,64,4,48]{3,2,1,0:T(4,128)(2,1)} %get-tuple-element.26.low_y, ...), custom_call_target="tpu_custom_call" | custom-call | tf_op jit(solution)/shard_map/halo/pallas_call | solution.py:291
  139.4 19.4 %transport.1 = f32[64,48,128]{2,1,0:T(8,128)} custom-call(f32[64,48,128]{2,1,0:T(8,128)} %get-tuple-element.23.s_ref, bf16[64,48,128]{2,1,0:T(8,128)(2,1)} %u_ref.3, bf16[64,48,128]{2,1,0:T(8,128)(2,1)} %v_ref.3, bf16[2,3,64,4,128]{4,3,2,1,0:T(4,128)(2,1)} %get-tuple-element.28.hx_ref, bf16[3,2,3,64,4,48]{5,4,3,2,1,0:T(4,128)(2,1)} %get-tuple-element.29.hy_ref), custom_call_target="tpu_custom_call" | custom-call | tf_op jit(solution)/shard_map/transport/pallas_call | solution.py:780
  (5 shorter events, 0.1 us)

commit v2 on v1

--- a/solution.py
+++ b/solution.py
@@ -7,8 +7,6 @@
 from jax.sharding import PartitionSpec as P
 
 HALO = 3
-STRIP = 4
-EDGE = 8
 CODE = 32767.0
 highest = lax.Precision.HIGHEST
 
@@ -220,99 +218,151 @@
     return [(dx, dy) for dx in (-1, 0, 1) for dy in (-1, 0, 1) if (dx, dy) != (0, 0)]
 
 
-def halo_kernel(low_x, high_x, low_y, high_y, from_x, from_y, send_sem, recv_sem):
-    gx, gy = lax.axis_index("gx"), lax.axis_index("gy")
-    size_x, size_y = lax.axis_size("gx"), lax.axis_size("gy")
-    barrier = pltpu.get_barrier_semaphore()
-
-    def present(dx, dy):
-        x, y = gx + dx, gy + dy
-        return (x >= 0) & (x < size_x) & (y >= 0) & (y < size_y)
-
-    def copy(k, dx, dy):
-        if dy == 0:
-            source = high_x if dx == 1 else low_x
-            target = from_x.at[0 if dx == 1 else 1]
+class Edges:
+    def __init__(self, edge_ref, strip_ref, rows_ref, strips_ref, sems):
+        self.refs = edge_ref, strip_ref, rows_ref, strips_ref
+        self.sems = sems
+        self.at = lax.axis_index("gx"), lax.axis_index("gy")
+        self.size = lax.axis_size("gx"), lax.axis_size("gy")
+
+    def present(self, dx, dy):
+        x, y = self.at[0] + dx, self.at[1] + dy
+        return (x >= 0) & (x < self.size[0]) & (y >= 0) & (y < self.size[1])
+
+    def copies(self, k, dx, dy):
+        edge_ref, strip_ref, rows_ref, strips_ref = self.refs
+        cx = strip_ref.shape[1]
+        slot = 1 - dy
+        if dx == 0:
+            pairs = [(strip_ref, strips_ref.at[slot, :, pl.ds(HALO, cx)])]
         else:
-            source = high_y if dy == 1 else low_y
-            target = from_y.at[1 - dx, 0 if dy == 1 else 1]
-        return pltpu.make_async_remote_copy(
-            src_ref=source,
-            dst_ref=target,
-            send_sem=send_sem.at[k],
-            recv_sem=recv_sem.at[k],
-            device_id={"gx": gx + dx, "gy": gy + dy},
-            device_id_type=pl.DeviceIdType.MESH,
-        )
-
-    around = 0
-    for dx, dy in ways():
-        around = around + present(dx, dy).astype(jnp.int32)
-
-        @pl.when(present(dx, dy))
-        def _():
-            pl.semaphore_signal(
-                barrier,
-                inc=1,
-                device_id={"gx": gx + dx, "gy": gy + dy},
+            first = cx - HALO if dx == 1 else 0
+            target = 0 if dx == 1 else cx + HALO
+            pairs = [
+                (
+                    strip_ref.at[:, pl.ds(first, HALO)],
+                    strips_ref.at[slot, :, pl.ds(target, HALO)],
+                )
+            ]
+            if dy == 0:
+                side = 0 if dx == 1 else 1
+                pairs.append((edge_ref.at[1 - side], rows_ref.at[side]))
+        return [
+            pltpu.make_async_remote_copy(
+                src_ref=source,
+                dst_ref=target,
+                send_sem=self.sems.at[0, j, k],
+                recv_sem=self.sems.at[1, j, k],
+                device_id={"gx": self.at[0] + dx, "gy": self.at[1] + dy},
                 device_id_type=pl.DeviceIdType.MESH,
             )
-
+            for j, (source, target) in enumerate(pairs)
+        ]
+
+    def greet(self, barrier):
+        around = 0
+        for dx, dy in ways():
+            here = self.present(dx, dy)
+            around = around + here.astype(jnp.int32)
+
+            @pl.when(here)
+            def _():
+                pl.semaphore_signal(
+                    barrier,
+                    inc=1,
+                    device_id={"gx": self.at[0] + dx, "gy": self.at[1] + dy},
+                    device_id_type=pl.DeviceIdType.MESH,
+                )
+
+        return around
+
+    def send(self):
+        _, strip_ref, rows_ref, strips_ref = self.refs
+        for k, (dx, dy) in enumerate(ways()):
+
+            @pl.when(self.present(dx, dy))
+            def _():
+                for copy in self.copies(k, dx, dy):
+                    copy.start()
+
+        cx = strip_ref.shape[1]
+        strips_ref[1, :, HALO : HALO + cx] = strip_ref[...]
+        for dx, dy in ways():
+            rows = HALO if dx else cx
+            first = HALO if dx == 0 else 0 if dx == 1 else cx + HALO
+
+            @pl.when(jnp.logical_not(self.present(-dx, -dy)))
+            def _():
+                blank = strips_ref[1 - dy, :, first : first + rows]
+                strips_ref[1 - dy, :, first : first + rows] = jnp.zeros(blank.shape, blank.dtype)
+                if dy == 0:
+                    side = 0 if dx == 1 else 1
+                    rows_ref[side] = jnp.zeros(rows_ref.shape[1:], rows_ref.dtype)
+
+    def finish(self):
+        for k, (dx, dy) in enumerate(ways()):
+
+            @pl.when(self.present(dx, dy))
+            def _():
+                for copy in self.copies(k, dx, dy):
+                    copy.wait_send()
+
+            @pl.when(self.present(-dx, -dy))
+            def _():
+                for copy in self.copies(k, dx, dy):
+                    copy.wait_recv()
+
+
+def edge_shapes(arrays, lev, cx, cy):
+    return [
+        jax.ShapeDtypeStruct((2, arrays, HALO, lev, cy), jnp.bfloat16),
+        jax.ShapeDtypeStruct((3, arrays, cx + 2 * HALO, 8, cy), jnp.bfloat16),
+    ]
+
+
+def halo_kernel(edge_ref, strip_ref, rows_ref, strips_ref, sems):
+    edges = Edges(edge_ref, strip_ref, rows_ref, strips_ref, sems)
+    barrier = pltpu.get_barrier_semaphore()
+    around = edges.greet(barrier)
     pl.semaphore_wait(barrier, around)
-    for k, (dx, dy) in enumerate(ways()):
-
-        @pl.when(present(dx, dy))
-        def _():
-            copy(k, dx, dy).start()
-
-    for k, (dx, dy) in enumerate(ways()):
-
-        @pl.when(jnp.logical_not(present(-dx, -dy)))
-        def _():
-            if dy == 0:
-                slot = 0 if dx == 1 else 1
-                from_x[slot] = jnp.zeros(from_x.shape[1:], from_x.dtype)
-            else:
-                slot = 0 if dy == 1 else 1
-                from_y[1 - dx, slot] = jnp.zeros(from_y.shape[2:], from_y.dtype)
-
-    for k, (dx, dy) in enumerate(ways()):
-
-        @pl.when(present(dx, dy))
-        def _():
-            copy(k, dx, dy).wait_send()
-
-        @pl.when(present(-dx, -dy))
-        def _():
-            copy(k, dx, dy).wait_recv()
-
-
-def halo(low_x, high_x, low_y, high_y, collective_id):
-    return pl.pallas_call(
-        halo_kernel,
-        out_shape=[
-            jax.ShapeDtypeStruct((2,) + low_x.shape, low_x.dtype),
-            jax.ShapeDtypeStruct((3, 2) + low_y.shape, low_y.dtype),
-        ],
-        in_specs=[pl.BlockSpec(memory_space=pltpu.VMEM)] * 4,
-        out_specs=[pl.BlockSpec(memory_space=pltpu.VMEM)] * 2,
-        scratch_shapes=[pltpu.SemaphoreType.DMA((8,)), pltpu.SemaphoreType.DMA((8,))],
-        compiler_params=pltpu.CompilerParams(
-            collective_id=collective_id, has_side_effects=True
-        ),
-        name="halo",
-    )(low_x, high_x, low_y, high_y)
-
-
-def edge_columns(cy, width):
-    row = lax.broadcasted_iota(jnp.int32, (2 * width, cy), 0)
-    col = lax.broadcasted_iota(jnp.int32, (2 * width, cy), 1)
-    return (col == jnp.where(row < width, row, row + cy - 2 * width)).astype(jnp.bfloat16)
+    edges.send()
+    edges.finish()
+
+
+def put_strip(turned_ref, strip_ref, w, group):
+    width = turned_ref.shape[1] // pl.num_programs(0)
+    value = turned_ref[...]
+    lane = lax.broadcasted_iota(jnp.int32, value.shape, 1)
+    first = group * width
+    moved = pltpu.roll(value, first + width // 4, 1)
+    here = (lane >= first) & (lane < first + width // 2)
+    strip_ref[w] = jnp.where(here, moved, strip_ref[w])
+
+
+def turn(value_ref, out_ref, edge_ref, strips_ref, turned_ref, strip_ref, w, group):
+    levels, cx, cy = value_ref.shape
+    for l in range(levels):
+        turned_ref[pl.ds(l, cx, stride=levels), :] = value_ref[l].astype(jnp.float32)
+    turned = turned_ref[...].reshape(cx, levels, cy)
+    out_ref[...] = turned.astype(out_ref.dtype)
+    edge_ref[0, w] = turned[:HALO].astype(edge_ref.dtype)
+    edge_ref[1, w] = turned[cx - HALO :].astype(edge_ref.dtype)
+
+    @pl.when(group == 0)
+    def _():
+        strip_ref[w] = jnp.zeros(strip_ref.shape[1:], strip_ref.dtype)
+
+    put_strip(turned_ref, strip_ref, w, group)
+
+    @pl.when(group == pl.num_programs(0) - 1)
+    def _():
+        strips_ref[w] = strip_ref[w].reshape(cx, levels, cy).astype(strips_ref.dtype)
 
 
 def fields_kernel(
-    members, most, note_ref, got_ref, c_ref, e_ref, coef_ref,
-    x_ref, state_ref, sum_ref, ens_ref, run_ref,
+    members, most, note_ref, got_ref, c_ref, e_ref, coef_ref, u_ref, v_ref,
+    x_ref, state_ref, ut_ref, vt_ref, edge_ref, strips_ref,
+    sum_ref, ens_ref, run_ref, turned_ref, strip_ref,
 ):
     _, levels, cx, cy = e_ref.shape
     lev = c_ref.shape[1]
@@ -324,6 +374,8 @@
     def _():
         home_sums(most, note_ref, got_ref, c_ref, sum_ref)
 
+    for w, (wind_ref, wt_ref) in enumerate(((u_ref, ut_ref), (v_ref, vt_ref))):
+        turn(wind_ref, wt_ref, edge_ref, strips_ref, turned_ref, strip_ref, w, i)
     for m in range(members):
         for l in range(levels):
             start = (m * levels + l) * cx
@@ -476,7 +528,10 @@
     state_ref[...] = rows_ref[...].astype(state_ref.dtype)
 
 
-def carry_y_kernel(cells, s_ref, coef_ref, o_ref, in_ref, sems):
+def carry_y_kernel(
+    cells, s_ref, coef_ref, edge_ref, strip_ref, o_ref, rows_ref, strips_ref, in_ref, sems, more
+):
+    edges = Edges(edge_ref, strip_ref, rows_ref, strips_ref, more)
     size = lax.axis_size("gy")
     me = lax.axis_index("gy")
     _, lev, width = s_ref.shape
@@ -488,8 +543,9 @@
             device_id={"gy": lax.rem(me + k, size)},
             device_id_type=pl.DeviceIdType.MESH,
         )
+    around = edges.greet(barrier)
     in_ref[me] = s_ref[...]
-    pl.semaphore_wait(barrier, size - 1)
+    pl.semaphore_wait(barrier, size - 1 + around)
 
     def copy(to, slot):
         return pltpu.make_async_remote_copy(
@@ -503,6 +559,7 @@
 
     for k in range(1, size):
         copy(lax.rem(me + k, size), me).start()
+    edges.send()
     for k in range(1, size):
         peer = lax.rem(me + k, size)
         landed = copy(peer, peer)
@@ -526,6 +583,7 @@
         leave = in_ref[t, 1].astype(jnp.float32) + link * entered[t] + step * leave
     o_ref[0] = mine
     o_ref[1] = last
+    edges.finish()
 
 
 def ends_of(first, second):
@@ -536,11 +594,10 @@
 
 
 def final_kernel(
-    members, z_ref, y_ref, coef_ref, u_ref, v_ref,
-    a_ref, s_ref, low_x, high_x, low_y, high_y,
+    members, z_ref, y_ref, coef_ref,
+    a_ref, s_ref, edge_ref, strips_ref, static_ref, turned_ref, strip_ref,
 ):
     _, levels, cx, cy = a_ref.shape
-    columns = edge_columns(cy, STRIP)
     along = lax.broadcasted_iota(jnp.int32, (1, cy), 1).astype(jnp.float32)
     for l in range(levels):
         rate = coef_ref[0, l : l + 1, :]
@@ -558,61 +615,81 @@
             (((0,), (0,)), ((), ())),
             preferred_element_type=jnp.float32,
         )
-        static = field[:cx]
-        s_ref[l] = static
+        static_ref[l] = field[:cx]
         for m in range(members):
             a_ref[m, l] = field[(m + 1) * cx : (m + 2) * cx]
-        for k, value in enumerate((static.astype(jnp.bfloat16), u_ref[l], v_ref[l])):
-            low_x[k, l] = value[:STRIP]
-            high_x[k, l] = value[cx - STRIP :]
-            sides = lax.dot_general(
-                columns, value, (((1,), (1,)), ((), ())), preferred_element_type=jnp.float32
+    turn(
+        static_ref, s_ref, edge_ref, strips_ref, turned_ref, strip_ref, 0, pl.program_id(0)
+    )
+
+
+def transport_kernel(
+    s_ref, ut_ref, vt_ref, srow_ref, sstrip_ref, wrow_ref, wstrip_ref, o_ref,
+    side_ref, lead_ref, s_buf, u_buf, v_buf,
+):
+    cx, levels, cy = s_ref.shape
+    total = cx + 2 * HALO
+    group = pl.program_id(0)
+    width = cy // pl.num_programs(0)
+    lane = lax.broadcasted_iota(jnp.int32, (levels, cy), 1)
+    part = lax.rem(lane, width)
+    quarter = width // 4
+
+    def along_x(before, here, after, wind):
+        return here + jnp.abs(wind) * (jnp.where(wind > 0.0, before, after) - here)
+
+    def along_y(before, here, after, wind):
+        return here + jnp.abs(wind) * (jnp.where(wind > 0.0, before, after) - here)
+
+    @pl.when(group == 0)
+    def _():
+        def place(x, _):
+            for j, (ref, w) in enumerate(((sstrip_ref, 0), (wstrip_ref, 0), (wstrip_ref, 1))):
+                left, own, right = [ref[k, w, x].astype(jnp.float32) for k in range(3)]
+                far = pltpu.roll(jnp.where(part < quarter, own, right), 2 * quarter, 1)
+                side_ref[j, x] = jnp.where(
+                    part < quarter, left, jnp.where(part < 2 * quarter, own, far)
+                )
+            return 0
+
+        lax.fori_loop(0, total, place, 0)
+        for p in range(HALO):
+            before = side_ref[0, p]
+            for x in range(p + 1, total - 1 - p):
+                here = side_ref[0, x]
+                value = along_x(before, here, side_ref[0, x + 1], side_ref[1, x])
+                before = here
+                lead_ref[p, x] = jnp.where(
+                    part == quarter - 2, pltpu.roll(value, cy - 2 * quarter - 2, 1), value
+                )
+                side_ref[0, x] = along_y(
+                    pltpu.roll(value, 1, 1), value, pltpu.roll(value, cy - 1, 1), side_ref[2, x]
+                )
+
+    for buf, center, row_ref, w in (
+        (s_buf, s_ref, srow_ref, 0), (u_buf, ut_ref, wrow_ref, 0), (v_buf, vt_ref, wrow_ref, 1)
+    ):
+        buf[:HALO] = row_ref[0, w].astype(jnp.float32)
+        buf[HALO : HALO + cx] = center[...].astype(jnp.float32)
+        buf[HALO + cx :] = row_ref[1, w].astype(jnp.float32)
+    shift = cy - (group * width + quarter - 1)
+    for p in range(HALO):
+        before = s_buf[p]
+        for x in range(p + 1, total - 1 - p):
+            here = s_buf[x]
+            value = along_x(before, here, s_buf[x + 1], u_buf[x])
+            before = here
+            lead = pltpu.roll(lead_ref[p, x], shift, 1)
+            value = along_y(
+                jnp.where(lane == 0, lead, pltpu.roll(value, 1, 1)),
+                value,
+                jnp.where(lane == cy - 1, lead, pltpu.roll(value, cy - 1, 1)),
+                v_buf[x],
             )
-            low_y[k, l] = sides[:STRIP].astype(low_y.dtype)
-            high_y[k, l] = sides[STRIP:].astype(high_y.dtype)
-
-
-def transport_kernel(s_ref, u_ref, v_ref, hx_ref, hy_ref, o_ref):
-    levels, cx, cy = o_ref.shape
-    rows, lanes = cx + 2 * EDGE, 2 * cy
-    blank = jnp.zeros((EDGE - STRIP, cy), jnp.float32)
-    place = edge_columns(cy, STRIP)
-
-    def widened(value, k, l):
-        strips = []
-        for j in range(3):
-            pair = jnp.concatenate(
-                [
-                    hy_ref[j, 1, k, l].astype(jnp.float32),
-                    hy_ref[j, 0, k, l].astype(jnp.float32),
-                ],
-                axis=0,
-            ).astype(jnp.bfloat16)
-            strips.append(
-                lax.dot_general(
-                    pair, place, (((0,), (0,)), ((), ())), preferred_element_type=jnp.float32
-                )
-            )
-        above = hx_ref[0, k, l].astype(jnp.float32)
-        below = hx_ref[1, k, l].astype(jnp.float32)
-        return jnp.concatenate(
-            [
-                jnp.concatenate([blank, above, value, below, blank], axis=0),
-                jnp.concatenate([strips[0][cx - EDGE :], strips[1], strips[2][:EDGE]], axis=0),
-            ],
-            axis=1,
-        )
-
-    for l in range(levels):
-        s = widened(s_ref[l], 0, l)
-        u = widened(u_ref[l].astype(jnp.float32), 1, l)
-        v = widened(v_ref[l].astype(jnp.float32), 2, l)
-        east, north = u > 0.0, v > 0.0
-        u, v = jnp.abs(u), jnp.abs(v)
-        for _ in range(HALO):
-            s = s + u * (jnp.where(east, pltpu.roll(s, 1, 0), pltpu.roll(s, rows - 1, 0)) - s)
-            s = s + v * (jnp.where(north, pltpu.roll(s, 1, 1), pltpu.roll(s, lanes - 1, 1)) - s)
-        o_ref[l] = s[EDGE : EDGE + cx, :cy]
+            if p < HALO - 1:
+                s_buf[x] = value
+            else:
+                o_ref[pl.ds(x - HALO, levels, stride=cx), :] = value
 
 
 def body(
@@ -674,7 +751,7 @@
         dimension_semantics=("arbitrary",), vmem_limit_bytes=56 * 1024 * 1024
     )
     rows = fields * cx
-    local, state_x = pl.pallas_call(
+    local, state_x, turned_u, turned_v, wind_edge, wind_strip = pl.pallas_call(
         functools.partial(fields_kernel, members, most),
         grid=(steps,),
         in_specs=[
@@ -683,23 +760,35 @@
             whole(across),
             levels_second(members, cx, cy),
             levels_second(3, cy),
+            levels_first(cx, cy),
+            levels_first(cx, cy),
         ],
         out_specs=[
             pl.BlockSpec((tile * rows, cy), lambda i: (i, 0)),
             pl.BlockSpec((pieces, 2 * fields, part, cy), lambda i: (i, 0, 0, 0)),
+            levels_second(cx, cy),
+            levels_second(cx, cy),
+            pl.BlockSpec((2, 2, HALO, tile, cy), lambda i: (0, 0, 0, i, 0)),
+            pl.BlockSpec((2, cx, tile, cy), lambda i: (0, 0, 0, 0)),
         ],
         out_shape=[
             jax.ShapeDtypeStruct((lev * rows, cy), jnp.float32),
             jax.ShapeDtypeStruct((size_x, 2 * fields, part, cy), jnp.bfloat16),
+            jax.ShapeDtypeStruct((cx, lev, cy), jnp.bfloat16),
+            jax.ShapeDtypeStruct((cx, lev, cy), jnp.bfloat16),
+            jax.ShapeDtypeStruct((2, 2, HALO, lev, cy), jnp.bfloat16),
+            jax.ShapeDtypeStruct((2, cx, tile, cy), jnp.bfloat16),
         ],
         scratch_shapes=[
             pltpu.VMEM((cx * lev, cy), jnp.float32),
             pltpu.VMEM((members * tile * cx, cy), jnp.float32),
             pltpu.VMEM((rows, tile, cy), jnp.float32),
+            pltpu.VMEM((cx * tile, cy), jnp.float32),
+            pltpu.VMEM((2, cx * tile, cy), jnp.float32),
         ],
         compiler_params=params,
         name="fields",
-    )(note, got, across, ensemble, coef)
+    )(note, got, across, ensemble, coef, wind_u, wind_v)
     local = local.reshape(lev, rows, cy)
 
     vmem = pl.BlockSpec(memory_space=pltpu.VMEM)
@@ -733,65 +822,85 @@
         name="rows",
     )(local, swept, coef)
 
-    entered = pl.pallas_call(
+    entered, wind_rows, wind_strips = pl.pallas_call(
         functools.partial(carry_y_kernel, cy),
-        out_shape=jax.ShapeDtypeStruct((2, lev, rows), jnp.float32),
-        in_specs=[vmem, vmem],
-        out_specs=vmem,
+        out_shape=[jax.ShapeDtypeStruct((2, lev, rows), jnp.float32)]
+        + edge_shapes(2, lev, cx, cy),
+        in_specs=[vmem] * 4,
+        out_specs=[vmem] * 3,
         scratch_shapes=[
             pltpu.VMEM((size_y, 2, lev, rows), jnp.bfloat16),
             pltpu.SemaphoreType.DMA((2, size_y)),
+            pltpu.SemaphoreType.DMA((2, 2, 8)),
         ],
         compiler_params=pltpu.CompilerParams(collective_id=2, has_side_effects=True),
         name="carry_y",
-    )(state_y, coef)
-
-    grad_alpha, static, *strips = pl.pallas_call(
+    )(state_y, coef, wind_edge, wind_strip)
+
+    grad_alpha, static, edge, strip = pl.pallas_call(
         functools.partial(final_kernel, members),
         grid=(steps,),
-        in_specs=[
-            levels_first(rows, cy),
-            levels_second(2, rows),
-            levels_second(3, cy),
-            levels_first(cx, cy),
-            levels_first(cx, cy),
-        ],
+        in_specs=[levels_first(rows, cy), levels_second(2, rows), levels_second(3, cy)],
         out_specs=[
             levels_second(members, cx, cy),
-            levels_first(cx, cy),
-            levels_second(3, STRIP, cy),
-            levels_second(3, STRIP, cy),
-            levels_second(3, STRIP, cx),
-            levels_second(3, STRIP, cx),
+            levels_second(cx, cy),
+            pl.BlockSpec((2, 1, HALO, tile, cy), lambda i: (0, 0, 0, i, 0)),
+            pl.BlockSpec((1, cx, tile, cy), lambda i: (0, 0, 0, 0)),
         ],
         out_shape=[
             jax.ShapeDtypeStruct((members, lev, cx, cy), jnp.float32),
-            jax.ShapeDtypeStruct((lev, cx, cy), jnp.float32),
-            jax.ShapeDtypeStruct((3, lev, STRIP, cy), jnp.bfloat16),
-            jax.ShapeDtypeStruct((3, lev, STRIP, cy), jnp.bfloat16),
-            jax.ShapeDtypeStruct((3, lev, STRIP, cx), jnp.bfloat16),
-            jax.ShapeDtypeStruct((3, lev, STRIP, cx), jnp.bfloat16),
+            jax.ShapeDtypeStruct((cx, lev, cy), jnp.float32),
+            jax.ShapeDtypeStruct((2, 1, HALO, lev, cy), jnp.bfloat16),
+            jax.ShapeDtypeStruct((1, cx, tile, cy), jnp.bfloat16),
+        ],
+        scratch_shapes=[
+            pltpu.VMEM((tile, cx, cy), jnp.float32),
+            pltpu.VMEM((cx * tile, cy), jnp.float32),
+            pltpu.VMEM((1, cx * tile, cy), jnp.float32),
         ],
         compiler_params=params,
         name="final",
-    )(z, entered, coef, wind_u, wind_v)
-
-    halo_x, halo_y = halo(*strips, 5)
+    )(z, entered, coef)
+
+    edge_rows, edge_strips = pl.pallas_call(
+        halo_kernel,
+        out_shape=edge_shapes(1, lev, cx, cy),
+        in_specs=[vmem] * 2,
+        out_specs=[vmem] * 2,
+        scratch_shapes=[pltpu.SemaphoreType.DMA((2, 2, 8))],
+        compiler_params=pltpu.CompilerParams(collective_id=5, has_side_effects=True),
+        name="halo",
+    )(edge, strip)
+
+    def rows_of(array):
+        return pl.BlockSpec(array.shape[:3] + (tile, cy), lambda i: (0, 0, 0, i, 0))
+
+    extent = cx + 2 * HALO
     static = pl.pallas_call(
         transport_kernel,
         grid=(steps,),
         in_specs=[
-            levels_first(cx, cy),
-            levels_first(cx, cy),
-            levels_first(cx, cy),
-            pl.BlockSpec((2, 3, tile, STRIP, cy), lambda i: (0, 0, i, 0, 0)),
-            pl.BlockSpec((3, 2, 3, tile, STRIP, cx), lambda i: (0, 0, 0, i, 0, 0)),
-        ],
-        out_specs=levels_first(cx, cy),
-        out_shape=jax.ShapeDtypeStruct((lev, cx, cy), jnp.float32),
+            levels_second(cx, cy),
+            levels_second(cx, cy),
+            levels_second(cx, cy),
+            rows_of(edge_rows),
+            whole(edge_strips),
+            rows_of(wind_rows),
+            whole(wind_strips),
+        ],
+        out_specs=pl.BlockSpec((tile * cx, cy), lambda i: (i, 0)),
+        out_shape=jax.ShapeDtypeStruct((lev * cx, cy), jnp.float32),
+        scratch_shapes=[
+            pltpu.VMEM((3, extent, tile, cy), jnp.float32),
+            pltpu.VMEM((HALO, extent, tile, cy), jnp.float32),
+            pltpu.VMEM((extent, tile, cy), jnp.float32),
+            pltpu.VMEM((extent, tile, cy), jnp.float32),
+            pltpu.VMEM((extent, tile, cy), jnp.float32),
+        ],
         compiler_params=params,
         name="transport",
-    )(static, wind_u, wind_v, halo_x, halo_y)
+    )(static, turned_u, turned_v, edge_rows, edge_strips, wind_rows, wind_strips)
+    static = static.reshape(lev, cx, cy)
     return (grad_alpha, static)
 
 

time: 162 us -> 140 us (0.86); the launches traced: 159 us -> 138 us
  Pallas kernels: 149 us -> 129 us
    pallas_call x3, Pallas kernels: 49.6 us -> 31.4 us  [the longest x1 13.1 us: body(): pl.pallas_call(transport_kernel, grid=(steps,), in_specs=[levels_second(c...]
    pallas_call x1, Pallas kernels: 14.8 us -> 10.3 us  [body(): pl.pallas_call(functools.partial(final_kernel, members), grid=(steps,), i...]
    pallas_call x1, Pallas kernels: 16.9 us -> 19.1 us  [body(): pl.pallas_call(functools.partial(fields_kernel, members, most), grid=(ste...]
where the time goes in v2:
time: 140 us; the launch traced here: 138 us
  Pallas kernels  129 us (92%)
  local copies, waits for them, and re-layouts  5.53 us (4%)
  other arithmetic  3.66 us (3%)
    pallas_call x1, Pallas kernels, observe(): pl.pallas_call(functools.partial(obs_kernel, axes, most), out_shape=[jax....  41.3 us
    pallas_call x1, Pallas kernels, body(): pl.pallas_call(functools.partial(fields_kernel, members, most), grid=(ste...  19.1 us
    pallas_call x1, Pallas kernels, body(): pl.pallas_call(functools.partial(carry_x_kernel, cx), out_shape=jax.Shape...  15.5 us
    pallas_call x1, Pallas kernels, body(): pl.pallas_call(transport_kernel, grid=(steps,), in_specs=[levels_second(c...  13.1 us
    pallas_call x1, Pallas kernels, body(): pl.pallas_call(functools.partial(rows_kernel, fields), grid=(steps,), in_...  10.8 us
    pallas_call x1, Pallas kernels, body(): pl.pallas_call(functools.partial(final_kernel, members), grid=(steps,), i...  10.3 us
    pallas_call x1, Pallas kernels, body(): pl.pallas_call(functools.partial(carry_y_kernel, cy), out_shape=[jax.Shap...  9.72 us
    pallas_call x1, Pallas kernels, body(): pl.pallas_call(halo_kernel, out_shape=edge_shapes(1, lev, cx, cy), in_spe...  8.56 us

profile of v2, /device:TPU:0, one launch (start us, length us, event | category | flops | bytes accessed | tf_op | source)
XLA Modules:
  0.0 138.4 jit_solution(10360258032057261815)
XLA Ops:
  0.6 0.9 convert_reduce_fusion
  1.5 0.7 multiply_add_fusion
  2.2 1.4 select_reduce_fusion
  3.6 0.7 sqrt_multiply_fusion
  4.3 0.1 stack.26
  4.4 0.1 stack.25
  4.5 0.1 stack.24
  4.6 0.7 broadcast_bitcast_fusion.coef_ref
  5.3 0.7 broadcast_in_dim.42.coef_ref
  6.0 1.6 %copy.16 = bf16[1,512,64]{2,1,0:T(8,128)(2,1)} copy(bf16[1,512,64]{1,2,0:T(8,128)(2,1)} %param.16) | data formatting | bytes 131072 | tf_op args[5]
  7.6 2.2 %copy.20 = bf16[64,48,128]{2,0,1:T(8,128)(2,1)} copy(bf16[64,48,128]{2,1,0:T(8,128)(2,1)} %param.11) | data formatting | bytes 1572864 | tf_op args[0]
  9.9 41.3 %observe.1 = (s16[32,160,128]{2,1,0:T(8,128)(2,1)}, f32[32,1,128]{2,1,0:T(1,128)}) custom-call(s32[64]{0:T(128)} %get-tuple-element.42.order_ref, s32[64]{0:T(128)} %get-tuple-element.41.line_ref, s32[64]{0:T(128)} %get-tuple-element.40.count_ref, bf16[512,64]{1,0:T(8,128)(2,1)} %bitcast.15, f32[1,512]{1,0:T(1,128)} %w_ref.1, bf16[64,512,128]{2,1,0:T(8,128)(2,1)} %d_hbm.1), custom_call_target="tpu_custom_call" | custom-call | tf_op jit(solution)/shard_map/observe/pallas_call | solution.py:154
  51.2 19.1 %fields.1 = (f32[15360,128]{1,0:T(8,128)}, bf16[8,10,8,128]{3,2,1,0:T(8,128)(2,1)}, bf16[48,64,128]{2,1,0:T(8,128)(2,1)}, bf16[48,64,128]{2,1,0:T(8,128)(2,1)}, ...) custom-call(f32[32,1,128]{2,1,0:T(1,128)} %get-tuple-element.21.note_ref, ...), custom_call_target="tpu_custom_call" | custom-call | tf_op jit(solution)/shard_map/fields/pallas_call | solution.py:754
  70.3 15.5 %carry_x.1.enter_ref = f32[10,64,128]{2,1,0:T(8,128)} custom-call(bf16[8,10,8,128]{3,2,1,0:T(8,128)(2,1)} %get-tuple-element.24.s_ref, f32[8,3,8,128]{3,2,1,0:T(8,128)} %broadcast_bitcast_fusion.coef_ref), custom_call_target="tpu_custom_call" | custom-call | tf_op jit(solution)/shard_map/carry_x/pallas_call | solution.py:796
  85.8 10.8 %rows.1 = (f32[64,240,128]{2,1,0:T(8,128)}, bf16[2,64,240]{2,1,0:T(8,128)(2,1)}) custom-call(f32[64,240,128]{2,1,0:T(8,128)} %bitcast.12, f32[10,64,128]{2,1,0:T(8,128)} %carry_x.1.enter_ref, f32[3,64,128]{2,1,0:T(8,128)} %broadcast_in_dim.42.coef_ref), custom_call_target="tpu_custom_call" | custom-call | tf_op jit(solution)/shard_map/rows/pallas_call | solution.py:807
  96.7 9.7 %carry_y.1 = (f32[2,64,240]{2,1,0:T(8,128)}, bf16[2,2,3,64,128]{4,3,2,1,0:T(8,128)(2,1)}, bf16[3,2,54,8,128]{4,3,2,1,0:T(8,128)(2,1)}) custom-call(bf16[2,64,240]{2,1,0:T(8,128)(2,1)} %get-tuple-element.26.s_ref, f32[3,64,128]{2,1,0:T(8,128)} %broadcast_in_dim.42.coef_ref, bf16[2,2,3,64,128]{4,3,2,1,0:T(8,128)(2,1)} %get-tuple-element.27.edge_ref, ...), custom_call_target="tpu_custom_call" | custom-call | tf_op jit(solution)/shard_map/carry_y/pallas_call | solution.py:825
  106.4 10.3 %final.1 = (f32[4,64,48,128]{3,2,1,0:T(8,128)}, f32[48,64,128]{2,1,0:T(8,128)}, bf16[2,1,3,64,128]{4,3,2,1,0:T(8,128)(2,1)}, bf16[1,48,8,128]{3,2,1,0:T(8,128)(2,1)}) custom-call(f32[64,240,128]{2,1,0:T(8,128)} %get-tuple-element.25.z_ref, f32[2,64,240]{2,1,0:T(8,128)} %get-tuple-element.29.y_ref, f32[3,64,128]{2,1,0:T(8,128)} %broadcast_in_dim.42.coef_ref), custom_call_target="tpu_custom_call" | custom-call | tf_op jit(solution)/shard_map/final/pallas_call | solution.py:840
  116.7 8.6 %halo.1 = (bf16[2,1,3,64,128]{4,3,2,1,0:T(8,128)(2,1)}, bf16[3,1,54,8,128]{4,3,2,1,0:T(8,128)(2,1)}) custom-call(bf16[2,1,3,64,128]{4,3,2,1,0:T(8,128)(2,1)} %get-tuple-element.34.edge_ref, bf16[1,48,8,128]{3,2,1,0:T(8,128)(2,1)} %get-tuple-element.35.strip_ref), custom_call_target="tpu_custom_call" | custom-call | tf_op jit(solution)/shard_map/halo/pallas_call | solution.py:865
  125.3 13.1 %transport.1 = f32[3072,128]{1,0:T(8,128)} custom-call(f32[48,64,128]{2,1,0:T(8,128)} %get-tuple-element.31.s_ref, bf16[48,64,128]{2,1,0:T(8,128)(2,1)} %get-tuple-element.32.ut_ref, bf16[48,64,128]{2,1,0:T(8,128)(2,1)} %get-tuple-element.33.vt_ref, bf16[2,1,3,64,128]{4,3,2,1,0:T(8,128)(2,1)} %get-tuple-element.36.srow_ref, ...), custom_call_target="tpu_custom_call" | custom-call | tf_op jit(solution)/shard_map/transport/pallas_call | solution.py:879
  (5 shorter events, 0.1 us)

commit v3 on v2

--- a/solution.py
+++ b/solution.py
@@ -154,10 +154,10 @@
     return pl.pallas_call(
         functools.partial(obs_kernel, axes, most),
         out_shape=[
-            jax.ShapeDtypeStruct((count, rows, cy), jnp.int16),
-            jax.ShapeDtypeStruct((count, 1, cy), jnp.float32),
-        ],
-        in_specs=[smem, smem, smem, vmem, vmem, pl.BlockSpec(memory_space=pl.ANY)],
+            pltpu.VMEM((count, rows, cy), jnp.int16),
+            pltpu.VMEM((count, 1, cy), jnp.float32),
+        ],
+        in_specs=[smem, smem, smem, vmem, vmem, pl.BlockSpec(memory_space=pltpu.HBM)],
         out_specs=[vmem, vmem],
         scratch_shapes=[
             pltpu.VMEM((records, channels, cy), jnp.bfloat16),
@@ -171,10 +171,10 @@
         compiler_params=pltpu.CompilerParams(
             collective_id=collective_id,
             has_side_effects=True,
-            vmem_limit_bytes=56 * 1024 * 1024,
+            vmem_limit_bytes=24 * 1024 * 1024,
         ),
         name="observe",
-    )(order, lines, counts, jacobian, weight, departure)
+    )(order, lines, counts, jacobian, weight, pltpu.with_memory_space_constraint(departure, pltpu.HBM))
 
 
 def home_sums(most, note_ref, got_ref, c_ref, sum_ref):
@@ -315,8 +315,8 @@
 
 def edge_shapes(arrays, lev, cx, cy):
     return [
-        jax.ShapeDtypeStruct((2, arrays, HALO, lev, cy), jnp.bfloat16),
-        jax.ShapeDtypeStruct((3, arrays, cx + 2 * HALO, 8, cy), jnp.bfloat16),
+        pltpu.VMEM((2, arrays, HALO, lev, cy), jnp.bfloat16),
+        pltpu.VMEM((3, arrays, cx + 2 * HALO, 8, cy), jnp.bfloat16),
     ]
 
 
@@ -398,7 +398,8 @@
     for x in reversed(range(cx)):
         for k in range(fields):
             state[k] = run_ref[k * cx + x] + decay * state[k]
-            x_ref[pl.ds(k * cx + x, levels, stride=fields * cx), :] = state[k]
+            first = i * levels * fields * cx + k * cx + x
+            x_ref[pl.ds(first, levels, stride=fields * cx), :] = state[k]
     for j in range(pieces):
         for k in range(fields):
             state_ref[j, fields + k] = state[k][j * part : (j + 1) * part].astype(state_ref.dtype)
@@ -472,8 +473,10 @@
 
 
 def rows_kernel(fields, x_ref, enter_ref, coef_ref, z_ref, state_ref, rows_ref, far_ref, sum_ref):
-    levels, _, cy = z_ref.shape
-    cx = z_ref.shape[1] // fields
+    _, levels, _ = rows_ref.shape
+    _, cx, cy = z_ref.shape
+    cx = cx // fields
+    start = pl.program_id(0) * levels
     along = lax.broadcasted_iota(jnp.int32, (cx, cy), 0).astype(jnp.float32)
 
     @pl.when(pl.program_id(0) == 0)
@@ -494,7 +497,7 @@
         parts = []
         for k in range(fields):
             parts.append(
-                x_ref[l, k * cx : (k + 1) * cx, :]
+                x_ref[start + l, k * cx : (k + 1) * cx, :]
                 + ahead * enter_ref[k, l : l + 1, :]
                 + behind * enter_ref[fields + k, l : l + 1, :]
             )
@@ -516,7 +519,7 @@
             jnp.concatenate([high, low], axis=1), weights, preferred_element_type=jnp.float32
         )
         z = both[:, :cy] + both[:, cy:]
-        z_ref[l] = z
+        z_ref[start + l] = z
         ends = lax.dot_general(
             picks,
             z.astype(jnp.bfloat16),
@@ -609,7 +612,7 @@
         row, a, b, c, d = ends_of(y_ref[0, l : l + 1, :], y_ref[1, l : l + 1, :])
         down = jnp.where(row % 3 == 1, jnp.where(row < 3, b, d), jnp.where(row < 3, a, c))
         down = jnp.where(row < 6, down, 0.0)
-        field = z_ref[l] + lax.dot_general(
+        field = z_ref[pl.program_id(0) * levels + l] + lax.dot_general(
             down.astype(jnp.bfloat16),
             across.astype(jnp.bfloat16),
             (((0,), (0,)), ((), ())),
@@ -748,9 +751,10 @@
         )
 
     params = pltpu.CompilerParams(
-        dimension_semantics=("arbitrary",), vmem_limit_bytes=56 * 1024 * 1024
+        dimension_semantics=("arbitrary",), vmem_limit_bytes=32 * 1024 * 1024
     )
     rows = fields * cx
+    vmem = pl.BlockSpec(memory_space=pltpu.VMEM)
     local, state_x, turned_u, turned_v, wind_edge, wind_strip = pl.pallas_call(
         functools.partial(fields_kernel, members, most),
         grid=(steps,),
@@ -764,7 +768,7 @@
             levels_first(cx, cy),
         ],
         out_specs=[
-            pl.BlockSpec((tile * rows, cy), lambda i: (i, 0)),
+            vmem,
             pl.BlockSpec((pieces, 2 * fields, part, cy), lambda i: (i, 0, 0, 0)),
             levels_second(cx, cy),
             levels_second(cx, cy),
@@ -772,12 +776,12 @@
             pl.BlockSpec((2, cx, tile, cy), lambda i: (0, 0, 0, 0)),
         ],
         out_shape=[
-            jax.ShapeDtypeStruct((lev * rows, cy), jnp.float32),
-            jax.ShapeDtypeStruct((size_x, 2 * fields, part, cy), jnp.bfloat16),
-            jax.ShapeDtypeStruct((cx, lev, cy), jnp.bfloat16),
-            jax.ShapeDtypeStruct((cx, lev, cy), jnp.bfloat16),
-            jax.ShapeDtypeStruct((2, 2, HALO, lev, cy), jnp.bfloat16),
-            jax.ShapeDtypeStruct((2, cx, tile, cy), jnp.bfloat16),
+            pltpu.VMEM((lev * rows, cy), jnp.float32),
+            pltpu.VMEM((size_x, 2 * fields, part, cy), jnp.bfloat16),
+            pltpu.VMEM((cx, lev, cy), jnp.bfloat16),
+            pltpu.VMEM((cx, lev, cy), jnp.bfloat16),
+            pltpu.VMEM((2, 2, HALO, lev, cy), jnp.bfloat16),
+            pltpu.VMEM((2, cx, tile, cy), jnp.bfloat16),
         ],
         scratch_shapes=[
             pltpu.VMEM((cx * lev, cy), jnp.float32),
@@ -791,27 +795,28 @@
     )(note, got, across, ensemble, coef, wind_u, wind_v)
     local = local.reshape(lev, rows, cy)
 
-    vmem = pl.BlockSpec(memory_space=pltpu.VMEM)
     split_coef = jnp.moveaxis(coef.reshape(3, size_x, part, cy), 1, 0)
     swept = pl.pallas_call(
         functools.partial(carry_x_kernel, cx),
-        out_shape=jax.ShapeDtypeStruct((2 * fields, lev, cy), jnp.float32),
+        out_shape=pltpu.VMEM((2 * fields, lev, cy), jnp.float32),
         in_specs=[vmem, vmem],
         out_specs=vmem,
         scratch_shapes=[pltpu.VMEM(state_x.shape, jnp.bfloat16)] * 3
         + [pltpu.SemaphoreType.DMA((4, size_x))],
-        compiler_params=pltpu.CompilerParams(collective_id=1, has_side_effects=True),
+        compiler_params=pltpu.CompilerParams(
+            collective_id=1, has_side_effects=True, vmem_limit_bytes=12 * 1024 * 1024
+        ),
         name="carry_x",
     )(state_x, split_coef)
 
     z, state_y = pl.pallas_call(
         functools.partial(rows_kernel, fields),
         grid=(steps,),
-        in_specs=[levels_first(rows, cy), levels_second(2 * fields, cy), levels_second(3, cy)],
-        out_specs=[levels_first(rows, cy), levels_second(2, rows)],
+        in_specs=[vmem, levels_second(2 * fields, cy), levels_second(3, cy)],
+        out_specs=[vmem, levels_second(2, rows)],
         out_shape=[
-            jax.ShapeDtypeStruct((lev, rows, cy), jnp.float32),
-            jax.ShapeDtypeStruct((2, lev, rows), jnp.bfloat16),
+            pltpu.VMEM((lev, rows, cy), jnp.float32),
+            pltpu.VMEM((2, lev, rows), jnp.bfloat16),
         ],
         scratch_shapes=[
             pltpu.VMEM((2, tile, rows), jnp.float32),
@@ -824,7 +829,7 @@
 
     entered, wind_rows, wind_strips = pl.pallas_call(
         functools.partial(carry_y_kernel, cy),
-        out_shape=[jax.ShapeDtypeStruct((2, lev, rows), jnp.float32)]
+        out_shape=[pltpu.VMEM((2, lev, rows), jnp.float32)]
         + edge_shapes(2, lev, cx, cy),
         in_specs=[vmem] * 4,
         out_specs=[vmem] * 3,
@@ -833,14 +838,16 @@
             pltpu.SemaphoreType.DMA((2, size_y)),
             pltpu.SemaphoreType.DMA((2, 2, 8)),
         ],
-        compiler_params=pltpu.CompilerParams(collective_id=2, has_side_effects=True),
+        compiler_params=pltpu.CompilerParams(
+            collective_id=2, has_side_effects=True, vmem_limit_bytes=12 * 1024 * 1024
+        ),
         name="carry_y",
     )(state_y, coef, wind_edge, wind_strip)
 
     grad_alpha, static, edge, strip = pl.pallas_call(
         functools.partial(final_kernel, members),
         grid=(steps,),
-        in_specs=[levels_first(rows, cy), levels_second(2, rows), levels_second(3, cy)],
+        in_specs=[vmem, levels_second(2, rows), levels_second(3, cy)],
         out_specs=[
             levels_second(members, cx, cy),
             levels_second(cx, cy),
@@ -849,9 +856,9 @@
         ],
         out_shape=[
             jax.ShapeDtypeStruct((members, lev, cx, cy), jnp.float32),
-            jax.ShapeDtypeStruct((cx, lev, cy), jnp.float32),
-            jax.ShapeDtypeStruct((2, 1, HALO, lev, cy), jnp.bfloat16),
-            jax.ShapeDtypeStruct((1, cx, tile, cy), jnp.bfloat16),
+            pltpu.VMEM((cx, lev, cy), jnp.float32),
+            pltpu.VMEM((2, 1, HALO, lev, cy), jnp.bfloat16),
+            pltpu.VMEM((1, cx, tile, cy), jnp.bfloat16),
         ],
         scratch_shapes=[
             pltpu.VMEM((tile, cx, cy), jnp.float32),
@@ -868,7 +875,9 @@
         in_specs=[vmem] * 2,
         out_specs=[vmem] * 2,
         scratch_shapes=[pltpu.SemaphoreType.DMA((2, 2, 8))],
-        compiler_params=pltpu.CompilerParams(collective_id=5, has_side_effects=True),
+        compiler_params=pltpu.CompilerParams(
+            collective_id=5, has_side_effects=True, vmem_limit_bytes=12 * 1024 * 1024
+        ),
         name="halo",
     )(edge, strip)
 

time: 140 us -> 117 us (0.84)
  Pallas kernels: 129 us -> 109 us
  local copies, waits for them, and re-layouts: 5.53 us -> 3.55 us
    pallas_call x3, Pallas kernels: 66.6 us -> 61.7 us  [the longest x1 39.8 us: observe(): pl.pallas_call(functools.partial(obs_kernel, axes, most), out_shape=[pltp...]
    pallas_call x1, Pallas kernels: 10.8 us -> 6.79 us  [body(): pl.pallas_call(functools.partial(rows_kernel, fields), grid=(steps,), in_...]
    pallas_call x1, Pallas kernels: 10.3 us -> 6.56 us  [body(): pl.pallas_call(functools.partial(final_kernel, members), grid=(steps,), i...]
    pallas_call x1, Pallas kernels: 19.1 us -> 16.3 us  [body(): pl.pallas_call(functools.partial(fields_kernel, members, most), grid=(ste...]
    pallas_call x1, Pallas kernels: 13.1 us -> 10.7 us  [body(): pl.pallas_call(transport_kernel, grid=(steps,), in_specs=[levels_second(c...]
    pallas_call x1, Pallas kernels: 8.56 us -> 6.51 us  [body(): pl.pallas_call(halo_kernel, out_shape=edge_shapes(1, lev, cx, cy), in_spe...]
    unnamed x2 -> x10, local copies, waits for them, and re-layouts: 3.81 us -> 3.14 us
where the time goes in v3:
time: 117 us; the launch traced here: 116 us
  Pallas kernels  109 us (93%)
  local copies, waits for them, and re-layouts  3.55 us (3%)
  other arithmetic  3.08 us (3%)
    pallas_call x1, Pallas kernels, observe(): pl.pallas_call(functools.partial(obs_kernel, axes, most), out_shape=[pltp...  39.8 us
    pallas_call x1, Pallas kernels, body(): pl.pallas_call(functools.partial(fields_kernel, members, most), grid=(ste...  16.3 us
    pallas_call x1, Pallas kernels, body(): pl.pallas_call(functools.partial(carry_x_kernel, cx), out_shape=pltpu.VME...  13.8 us
    pallas_call x1, Pallas kernels, body(): pl.pallas_call(transport_kernel, grid=(steps,), in_specs=[levels_second(c...  10.7 us
    pallas_call x1, Pallas kernels, body(): pl.pallas_call(functools.partial(carry_y_kernel, cy), out_shape=[pltpu.VM...  8.1 us
    pallas_call x1, Pallas kernels, body(): pl.pallas_call(functools.partial(rows_kernel, fields), grid=(steps,), in_...  6.79 us
    pallas_call x1, Pallas kernels, body(): pl.pallas_call(functools.partial(final_kernel, members), grid=(steps,), i...  6.56 us
    pallas_call x1, Pallas kernels, body(): pl.pallas_call(halo_kernel, out_shape=edge_shapes(1, lev, cx, cy), in_spe...  6.51 us

profile of v3, /device:TPU:0, one launch (start us, length us, event | category | flops | bytes accessed | tf_op | source)
XLA Modules:
  0.0 116.0 jit_solution(16928285833442641937)
XLA Ops:
  0.6 0.0 copy-start.1
  0.6 0.9 convert_reduce_fusion
  1.6 0.7 multiply_add_fusion
  2.2 0.8 select_reduce_fusion
  3.0 0.7 sqrt_multiply_fusion
  3.7 0.1 stack.26
  3.8 0.1 stack.25
  3.9 0.1 stack.24
  4.0 0.1 broadcast_bitcast_fusion.coef_ref
  4.1 0.1 broadcast_in_dim.42.coef_ref
  4.2 1.0 copy.16
  5.2 0.0 copy-start
  5.2 0.0 copy-start.2
  5.2 1.5 %copy.20 = bf16[64,48,128]{2,0,1:T(8,128)(2,1)S(1)} copy(bf16[64,48,128]{2,1,0:T(8,128)(2,1)} %param.11) | data formatting | bytes 1572864 | tf_op args[0]
  6.7 0.0 copy-start.3
  6.7 0.7 copy-done.3
  7.4 39.8 %observe.1 = (s16[32,160,128]{2,1,0:T(8,128)(2,1)S(1)}, f32[32,1,128]{2,1,0:T(1,128)S(1)}) custom-call(s32[64]{0:T(128)S(1)} %get-tuple-element.42.order_ref, s32[64]{0:T(128)S(1)} %get-tuple-element.41.line_ref, s32[64]{0:T(128)S(1)} %get-tuple-element.40.count_ref, bf16[512,64]{1,0:T(8,128)(2,1)S(1)} %bitcast.14, f32[1,512]{1,0:T(1,128)S(1)} %copy-done.3, ...), custom_call_target="tpu_custom_call" | custom-call | tf_op jit(solution)/shard_map/observe/pallas_call | solution.py:154
  47.2 0.0 copy-done.1
  47.2 0.0 copy-done
  47.2 0.0 copy-done.2
  47.2 16.3 %fields.1 = (f32[15360,128]{1,0:T(8,128)S(1)}, bf16[8,10,8,128]{3,2,1,0:T(8,128)(2,1)S(1)}, bf16[48,64,128]{2,1,0:T(8,128)(2,1)S(1)}, bf16[48,64,128]{2,1,0:T(8,...) custom-call(f32[32,1,128]{2,1,0:T(1,128)S(1)} %get-tuple-element.21.note_ref, ...), custom_call_target="tpu_custom_call" | custom-call | tf_op jit(solution)/shard_map/fields/pallas_call | solution.py:758
  63.5 13.8 %carry_x.1.enter_ref = f32[10,64,128]{2,1,0:T(8,128)S(1)} custom-call(bf16[8,10,8,128]{3,2,1,0:T(8,128)(2,1)S(1)} %get-tuple-element.24.s_ref, f32[8,3,8,128]{3,2,1,0:T(8,128)S(1)} %broadcast_bitcast_fusion.coef_ref), custom_call_target="tpu_custom_call" | custom-call | tf_op jit(solution)/shard_map/carry_x/pallas_call | solution.py:799
  77.3 6.8 %rows.1 = (f32[64,240,128]{2,1,0:T(8,128)S(1)}, bf16[2,64,240]{2,1,0:T(8,128)(2,1)S(1)}) custom-call(f32[64,240,128]{2,1,0:T(8,128)S(1)} %bitcast.12, f32[10,64,128]{2,1,0:T(8,128)S(1)} %carry_x.1.enter_ref, f32[3,64,128]{2,1,0:T(8,128)S(1)} %broadcast_in_dim.42.coef_ref), custom_call_target="tpu_custom_call" | custom-call | tf_op jit(solution)/shard_map/rows/pallas_call | solution.py:812
  84.1 8.1 %carry_y.1 = (f32[2,64,240]{2,1,0:T(8,128)S(1)}, bf16[2,2,3,64,128]{4,3,2,1,0:T(8,128)(2,1)S(1)}, bf16[3,2,54,8,128]{4,3,2,1,0:T(8,128)(2,1)S(1)}) custom-call(bf16[2,64,240]{2,1,0:T(8,128)(2,1)S(1)} %get-tuple-element.26.s_ref, f32[3,64,128]{2,1,0:T(8,128)S(1)} %broadcast_in_dim.42.coef_ref, bf16[2,2,3,64,128]{4,3,2,1,0:T(8,128)(2,1)S(1)} %get-tuple-element.27.edge_ref, ...), custom_call_target="tpu_custom_call" | custom-call | tf_op jit(solution)/shard_map/carry_y/pallas_call | solution.py:830
  92.2 6.6 %final.1 = (f32[4,64,48,128]{3,2,1,0:T(8,128)}, f32[48,64,128]{2,1,0:T(8,128)S(1)}, bf16[2,1,3,64,128]{4,3,2,1,0:T(8,128)(2,1)S(1)}, bf16[1,48,8,128]{3,2,1,0:T(8,128)(2,1)S(1)}) custom-call(f32[64,240,128]{2,1,0:T(8,128)S(1)} %get-tuple-element.25.z_ref, f32[2,64,240]{2,1,0:T(8,128)S(1)} %get-tuple-element.29.y_ref, f32[3,64,128]{2,1,0:T(8,128)S(1)} %broadcast_in_dim.42.coef_ref), custom_call_target="tpu_custom_call" | custom-call | tf_op jit(solution)/shard_map/final/pallas_call | solution.py:847
  98.8 6.5 %halo.1 = (bf16[2,1,3,64,128]{4,3,2,1,0:T(8,128)(2,1)S(1)}, bf16[3,1,54,8,128]{4,3,2,1,0:T(8,128)(2,1)S(1)}) custom-call(bf16[2,1,3,64,128]{4,3,2,1,0:T(8,128)(2,1)S(1)} %get-tuple-element.34.edge_ref, bf16[1,48,8,128]{3,2,1,0:T(8,128)(2,1)S(1)} %get-tuple-element.35.strip_ref), custom_call_target="tpu_custom_call" | custom-call | tf_op jit(solution)/shard_map/halo/pallas_call | solution.py:872
  105.3 10.7 %transport.1 = f32[3072,128]{1,0:T(8,128)} custom-call(f32[48,64,128]{2,1,0:T(8,128)S(1)} %get-tuple-element.31.s_ref, bf16[48,64,128]{2,1,0:T(8,128)(2,1)S(1)} %get-tuple-element.32.ut_ref, bf16[48,64,128]{2,1,0:T(8,128)(2,1)S(1)} %get-tuple-element.33.vt_ref, bf16[2,1,3,64,128]{4,3,2,1,0:T(8,128)(2,1)S(1)} %get-tuple-element.36.srow_ref, ...), custom_call_target="tpu_custom_call" | custom-call | tf_op jit(solution)/shard_map/transport/pallas_call | solution.py:888
  (5 shorter events, 0.1 us)
Async XLA Ops:
  0.6 46.5 %copy-start.1 = (bf16[64,48,128]{2,1,0:T(8,128)(2,1)S(1)}, bf16[64,48,128]{2,1,0:T(8,128)(2,1)}, u32[]{:S(2)}) copy-start(bf16[64,48,128]{2,1,0:T(8,128)(2,1)} %u_ref.1) | copy-start | bytes 2359300
  5.2 42.0 %copy-start = (bf16[4,64,48,128]{3,2,1,0:T(8,128)(2,1)S(1)}, bf16[4,64,48,128]{3,2,1,0:T(8,128)(2,1)}, u32[]{:S(2)}) copy-start(bf16[4,64,48,128]{3,2,1,0:T(8,128)(2,1)} %e_ref.1) | copy-start | bytes 9437188
  5.2 42.0 %copy-start.2 = (bf16[64,48,128]{2,1,0:T(8,128)(2,1)S(1)}, bf16[64,48,128]{2,1,0:T(8,128)(2,1)}, u32[]{:S(2)}) copy-start(bf16[64,48,128]{2,1,0:T(8,128)(2,1)} %v_ref.1) | copy-start | bytes 2359300
  6.7 0.7 copy-start.3

commit v4 on v3

--- a/solution.py
+++ b/solution.py
@@ -38,15 +38,18 @@
 
 
 def obs_kernel(
-    axes, most, order_ref, line_ref, count_ref, j_ref, w_ref, d_hbm, got_ref, note_ref,
-    d_buf, send_buf, note_buf, lhs_ref, hold_ref, scale_ref,
-    d_sem, send_sem, recv_sem, note_send, note_recv,
+    axes, most, order_ref, line_ref, count_ref, j_ref, w_ref, d_hbm, c_ref, sum_ref, note_ref,
+    d_buf, send_buf, got_ref, scale_buf, scale_ref, note_buf, note_smem, lhs_ref, hold_ref,
+    gram_ref, gain_ref, d_sem, sems, gram_sem, smem_sem,
 ):
     count = lax.axis_size(axes)
+    size_x, size_y = lax.axis_size("gx"), lax.axis_size("gy")
+    at_x, at_y = lax.axis_index("gx"), lax.axis_index("gy")
     half = count // 2
     me = position(axes)
     lev = j_ref.shape[1]
     cy = d_buf.shape[2]
+    mesh_id = pl.DeviceIdType.MESH
     barrier = pltpu.get_barrier_semaphore()
     pieces = d_sem.shape[0]
     size = d_buf.shape[0] // pieces
@@ -63,39 +66,92 @@
             barrier,
             inc=1,
             device_id=peer_id(axes, lax.rem(me + k, count)),
-            device_id_type=pl.DeviceIdType.MESH,
+            device_id_type=mesh_id,
         )
         return 0
 
     lax.fori_loop(1, count, greet, 0)
+    lane = lax.broadcasted_iota(jnp.int32, (1, cy), 1)
+
+    def words(home, _):
+        word = jnp.zeros((1, cy), jnp.int32)
+        for m in range(most):
+            word = jnp.where(lane == m, line_ref[home * most + m], word)
+            word = jnp.where(lane == most + m, count_ref[home * most + m], word)
+        note_buf[home] = word
+        return 0
+
+    lax.fori_loop(0, count, words, 0)
     turned = j_ref[...].astype(jnp.float32).T
     high, low = split(turned * w_ref[...])
     lhs_ref[...] = jnp.concatenate([high, low], axis=0)
     both = jnp.dot(lhs_ref[...], j_ref[...], preferred_element_type=jnp.float32)
     normal = both[:lev] + both[lev:]
-    code, scale = coded(normal)
+    code, gain = coded(normal)
     hold_ref[...] = jnp.concatenate([code[: lev // 2], code[lev // 2 :]], axis=1)
-    scale_ref[...] = jnp.broadcast_to(scale, scale_ref.shape)
+    gain_ref[...] = jnp.broadcast_to(gain, gain_ref.shape)
+    gram_ref[at_y, at_x] = hold_ref[...]
+    note_ref[me] = note_buf[me]
+    pl.semaphore_wait(barrier, count - 1)
+
+    def remote(kind, source, target, to, slot):
+        return pltpu.make_async_remote_copy(
+            src_ref=source,
+            dst_ref=target,
+            send_sem=sems.at[kind, to],
+            recv_sem=sems.at[kind + 1, slot],
+            device_id=peer_id(axes, to),
+            device_id_type=mesh_id,
+        )
+
+    def notes(to, slot):
+        return remote(4, note_buf.at[to], note_ref.at[slot], to, slot)
+
+    def gram_x(to, slot):
+        return pltpu.make_async_remote_copy(
+            src_ref=hold_ref,
+            dst_ref=gram_ref.at[at_y, slot],
+            send_sem=gram_sem.at[0, to],
+            recv_sem=gram_sem.at[1, slot],
+            device_id={"gx": to},
+            device_id_type=mesh_id,
+        )
+
+    def gram_y(to, slot):
+        return pltpu.make_async_remote_copy(
+            src_ref=gram_ref.at[at_y],
+            dst_ref=gram_ref.at[slot],
+            send_sem=gram_sem.at[2, to],
+            recv_sem=gram_sem.at[3, slot],
+            device_id={"gy": to},
+            device_id_type=mesh_id,
+        )
+
+    def early(k, _):
+        gram_x(lax.rem(at_x + k, size_x), at_x).start()
+        return 0
+
+    def tell(k, _):
+        notes(lax.rem(me + k, count), me).start()
+        return 0
+
+    lax.fori_loop(1, size_x, early, 0)
+    lax.fori_loop(1, count, tell, 0)
     for i in range(pieces):
         piece(i).wait()
-    pl.semaphore_wait(barrier, count - 1)
-    lane = lax.broadcasted_iota(jnp.int32, (1, cy), 1)
-
-    def fill(home, target, note):
+
+    def fill(home, target, scale_row):
         blocks = [d_buf[order_ref[home * most + m]] for m in range(most)]
         both = jnp.dot(
             lhs_ref[...], jnp.concatenate(blocks, axis=1), preferred_element_type=jnp.float32
         )
-        word = jnp.where(lane == 3 * most, scale_ref[0:1, :], 0.0)
+        word = gain_ref[0:1, :]
         for m in range(most):
             part = both[:lev, m * cy : (m + 1) * cy] + both[lev:, m * cy : (m + 1) * cy]
             code, scale = coded(part)
             target[m * lev : (m + 1) * lev, :] = code
-            word = jnp.where(lane == m, line_ref[home * most + m].astype(jnp.float32), word)
-            word = jnp.where(lane == most + m, count_ref[home * most + m].astype(jnp.float32), word)
-            word = jnp.where(lane == 2 * most + m, scale, word)
-        target[most * lev :, :] = hold_ref[...]
-        note[...] = word
+            word = jnp.where(lane == m, scale, word)
+        scale_row[...] = word
 
     def goal(t):
         j = t + t // half
@@ -104,16 +160,9 @@
         return other * half + lax.rem(place + j, half)
 
     def sends(to, origin):
-        peer = dict(device_id=peer_id(axes, to), device_id_type=pl.DeviceIdType.MESH)
         return (
-            pltpu.make_async_remote_copy(
-                src_ref=send_buf.at[to], dst_ref=got_ref.at[origin],
-                send_sem=send_sem.at[to], recv_sem=recv_sem.at[origin], **peer
-            ),
-            pltpu.make_async_remote_copy(
-                src_ref=note_buf.at[to], dst_ref=note_ref.at[origin],
-                send_sem=note_send.at[to], recv_sem=note_recv.at[origin], **peer
-            ),
+            remote(0, send_buf.at[to], got_ref.at[origin], to, origin),
+            remote(2, scale_buf.at[to], scale_ref.at[origin], to, origin),
         )
 
     def begin(to):
@@ -121,97 +170,156 @@
             copy.start()
 
     first = goal(0)
-    fill(first, send_buf.at[first], note_buf.at[first])
+    fill(first, send_buf.at[first], scale_buf.at[first])
+    fill(me, got_ref.at[me], scale_ref.at[me])
+    begin(first)
 
     def step(t, _):
-        to = goal(t)
-        fill(to, send_buf.at[to], note_buf.at[to])
-        begin(goal(t - 1))
+        pair = [goal(2 * t + 1 + k) for k in range(2)]
+        for to in pair:
+            fill(to, send_buf.at[to], scale_buf.at[to])
+        for to in pair:
+            begin(to)
         return 0
 
-    lax.fori_loop(1, count - 1, step, 0)
-    fill(me, got_ref.at[me], note_ref.at[me])
-    begin(goal(count - 2))
-
-    def finish(k, _):
+    lax.fori_loop(0, half - 1, step, 0)
+
+    def landed_x(k, _):
+        peer = lax.rem(at_x + k, size_x)
+        gram_x(peer, peer).wait_send()
+        gram_x(peer, peer).wait_recv()
+        return 0
+
+    lax.fori_loop(1, size_x, landed_x, 0)
+    for k in range(1, size_y):
+        gram_y(lax.rem(at_y + k, size_y), at_y).start()
+
+    def told(k, _):
         peer = lax.rem(me + k, count)
+        notes(peer, peer).wait_send()
+        notes(peer, peer).wait_recv()
+        return 0
+
+    lax.fori_loop(1, count, told, 0)
+    to_smem = pltpu.make_async_copy(note_ref, note_smem, smem_sem)
+    to_smem.start()
+    to_smem.wait()
+    wide = lax.broadcasted_iota(jnp.int32, (lev // 2, 2 * lev), 1)
+
+    def product(at, k):
+        code = at.astype(jnp.int32).astype(jnp.float32)
+        high, low = split(code)
+        high, low = high.astype(jnp.float32), low.astype(jnp.float32)
+        matrix = jnp.concatenate(
+            [
+                jnp.where(wide < lev, high, pltpu.roll(low, lev, 1)),
+                jnp.where(wide < lev, pltpu.roll(high, lev, 1), low),
+            ],
+            axis=0,
+        ).astype(jnp.bfloat16)
+        block = jnp.concatenate([c_ref[note_smem[k, 0, m]] for m in range(most)], axis=1)
+        both = jnp.dot(
+            matrix, jnp.concatenate([block, block], axis=0), preferred_element_type=jnp.float32
+        )
+        for m in range(most):
+            sum_ref[k * most + m] = both[:, m * cy : (m + 1) * cy]
+
+    def products(y):
+        def four(x, _):
+            for k in range(4):
+                product(gram_ref[y, 4 * x + k], (4 * x + k) * size_y + y)
+            return 0
+
+        lax.fori_loop(0, size_x // 4, four, 0)
+
+    products(at_y)
+    for k in range(1, size_y):
+        peer = lax.rem(at_y + k, size_y)
+        gram_y(peer, peer).wait_send()
+        gram_y(peer, peer).wait_recv()
+        products(peer)
+    column = lax.broadcasted_iota(jnp.int32, (lev, cy), 1)
+
+    def settle(k):
+        scales = scale_ref[k]
+        for m in range(most):
+            part = got_ref[k, m * lev : (m + 1) * lev, :].astype(jnp.int32).astype(jnp.float32)
+            value = scales[:, most : most + 1] * sum_ref[k * most + m] - scales[:, m : m + 1] * part
+            sum_ref[k * most + m] = jnp.where(column < note_smem[k, 0, most + m], value, 0.0)
+
+    def wait(peer):
         for copy in sends(peer, peer):
             copy.wait_send()
             copy.wait_recv()
+
+    wait(first)
+    settle(me)
+    settle(first)
+
+    def finish(t, _):
+        pair = [goal(2 * t + 1 + k) for k in range(2)]
+        for peer in pair:
+            wait(peer)
+        for peer in pair:
+            settle(peer)
         return 0
 
-    lax.fori_loop(1, count, finish, 0)
-
-
-def observe(order, lines, counts, jacobian, weight, departure, axes, most, collective_id):
+    lax.fori_loop(0, half - 1, finish, 0)
+
+
+def observe(order, lines, counts, jacobian, weight, departure, across, axes, most, collective_id):
     count = lax.axis_size(axes)
+    size_x, size_y = lax.axis_size("gx"), lax.axis_size("gy")
     channels, lev = jacobian.shape
     records, _, cy = departure.shape
-    rows = most * lev + lev // 2
     smem = pl.BlockSpec(memory_space=pltpu.SMEM)
     vmem = pl.BlockSpec(memory_space=pltpu.VMEM)
     dma = pltpu.SemaphoreType.DMA
     return pl.pallas_call(
         functools.partial(obs_kernel, axes, most),
         out_shape=[
-            pltpu.VMEM((count, rows, cy), jnp.int16),
-            pltpu.VMEM((count, 1, cy), jnp.float32),
-        ],
-        in_specs=[smem, smem, smem, vmem, vmem, pl.BlockSpec(memory_space=pltpu.HBM)],
+            pltpu.VMEM((count * most, lev, cy), jnp.float32),
+            pltpu.VMEM((count, 1, cy), jnp.int32),
+        ],
+        in_specs=[smem, smem, smem, vmem, vmem, pl.BlockSpec(memory_space=pltpu.HBM), vmem],
         out_specs=[vmem, vmem],
         scratch_shapes=[
             pltpu.VMEM((records, channels, cy), jnp.bfloat16),
-            pltpu.VMEM((count, rows, cy), jnp.int16),
+            pltpu.VMEM((count, most * lev, cy), jnp.int16),
+            pltpu.VMEM((count, most * lev, cy), jnp.int16),
             pltpu.VMEM((count, 1, cy), jnp.float32),
+            pltpu.VMEM((count, 1, cy), jnp.float32),
+            pltpu.VMEM((count, 1, cy), jnp.int32),
+            pltpu.SMEM((count, 1, cy), jnp.int32),
             pltpu.VMEM((2 * lev, channels), jnp.bfloat16),
             pltpu.VMEM((lev // 2, 2 * lev), jnp.int16),
+            pltpu.VMEM((size_y, size_x, lev // 2, 2 * lev), jnp.int16),
             pltpu.VMEM((8, cy), jnp.float32),
-            dma((8,)), dma((count,)), dma((count,)), dma((count,)), dma((count,)),
+            dma((8,)), dma((6, count)), dma((4, max(size_x, size_y))), dma,
         ],
         compiler_params=pltpu.CompilerParams(
             collective_id=collective_id,
             has_side_effects=True,
-            vmem_limit_bytes=24 * 1024 * 1024,
+            vmem_limit_bytes=28 * 1024 * 1024,
         ),
         name="observe",
-    )(order, lines, counts, jacobian, weight, pltpu.with_memory_space_constraint(departure, pltpu.HBM))
-
-
-def home_sums(most, note_ref, got_ref, c_ref, sum_ref):
-    homes = got_ref.shape[0]
-    lev, cy = c_ref.shape[1:]
+    )(
+        order, lines, counts, jacobian, weight,
+        pltpu.with_memory_space_constraint(departure, pltpu.HBM), across,
+    )
+
+
+def home_sums(most, note_ref, got_ref, sum_ref):
+    slots, lev, _ = got_ref.shape
     sum_ref[...] = jnp.zeros(sum_ref.shape, sum_ref.dtype)
-    lane = lax.broadcasted_iota(jnp.int32, (lev // 2, 2 * lev), 1)
-    column = lax.broadcasted_iota(jnp.int32, (lev, cy), 1)
 
     def one(k, _):
-        code = got_ref[k, most * lev :, :].astype(jnp.int32).astype(jnp.float32)
-        high, low = split(code)
-        high, low = high.astype(jnp.float32), low.astype(jnp.float32)
-        matrix = jnp.concatenate(
-            [
-                jnp.where(lane < lev, high, pltpu.roll(low, lev, 1)),
-                jnp.where(lane < lev, pltpu.roll(high, lev, 1), low),
-            ],
-            axis=0,
-        ).astype(jnp.bfloat16)
-        lines = [note_ref[k, 0, m].astype(jnp.int32) for m in range(most)]
-        block = jnp.concatenate([c_ref[line] for line in lines], axis=1)
-        product = jnp.dot(
-            matrix, jnp.concatenate([block, block], axis=0), preferred_element_type=jnp.float32
-        )
         for m in range(most):
-            part = got_ref[k, m * lev : (m + 1) * lev, :].astype(jnp.int32).astype(jnp.float32)
-            value = (
-                note_ref[k, 0, 3 * most] * product[:, m * cy : (m + 1) * cy]
-                - note_ref[k, 0, 2 * most + m] * part
-            )
-            value = jnp.where(column < note_ref[k, 0, most + m].astype(jnp.int32), value, 0.0)
-            rows = pl.ds(pl.multiple_of(lines[m] * lev, lev), lev)
-            sum_ref[rows, :] += value
+            rows = pl.ds(pl.multiple_of(note_ref[k, 0, m] * lev, lev), lev)
+            sum_ref[rows, :] += got_ref[k * most + m]
         return 0
 
-    lax.fori_loop(0, homes, one, 0)
+    lax.fori_loop(0, slots // most, one, 0)
 
 
 def ways():
@@ -360,19 +468,19 @@
 
 
 def fields_kernel(
-    members, most, note_ref, got_ref, c_ref, e_ref, coef_ref, u_ref, v_ref,
+    members, most, note_ref, got_ref, e_ref, coef_ref, u_ref, v_ref,
     x_ref, state_ref, ut_ref, vt_ref, edge_ref, strips_ref,
     sum_ref, ens_ref, run_ref, turned_ref, strip_ref,
 ):
     _, levels, cx, cy = e_ref.shape
-    lev = c_ref.shape[1]
+    lev = got_ref.shape[1]
     fields = members + 1
     pieces, _, part, _ = state_ref.shape
     i = pl.program_id(0)
 
     @pl.when(i == 0)
     def _():
-        home_sums(most, note_ref, got_ref, c_ref, sum_ref)
+        home_sums(most, note_ref, got_ref, sum_ref)
 
     for w, (wind_ref, wt_ref) in enumerate(((u_ref, ut_ref), (v_ref, vt_ref))):
         turn(wind_ref, wt_ref, edge_ref, strips_ref, turned_ref, strip_ref, w, i)
@@ -724,10 +832,10 @@
         jnp.sum(jnp.where(placing, value[:, None], 0), axis=0)
         for value in (index, obs_line, obs_count)
     ]
+    across = jnp.transpose(increment, (1, 0, 2))
     got, note = observe(
-        order, lines, counts, jacobian[0], obs_weight, departure, axes, most, 3
+        order, lines, counts, jacobian[0], obs_weight, departure, across, axes, most, 3
     )
-    across = jnp.transpose(increment, (1, 0, 2))
     rate = -1.0 / filter_length
     tall = -1.0 / jnp.expm1(2.0 * rate)
     gain = -jnp.expm1(rate) * jnp.sqrt(-jnp.expm1(2.0 * rate))
@@ -760,8 +868,7 @@
         grid=(steps,),
         in_specs=[
             pl.BlockSpec(memory_space=pltpu.SMEM),
-            whole(got),
-            whole(across),
+            vmem,
             levels_second(members, cx, cy),
             levels_second(3, cy),
             levels_first(cx, cy),
@@ -792,7 +899,7 @@
         ],
         compiler_params=params,
         name="fields",
-    )(note, got, across, ensemble, coef, wind_u, wind_v)
+    )(note, got, ensemble, coef, wind_u, wind_v)
     local = local.reshape(lev, rows, cy)
 
     split_coef = jnp.moveaxis(coef.reshape(3, size_x, part, cy), 1, 0)

time: 117 us -> 108 us (0.923)
  Pallas kernels: 109 us -> 101 us
    pallas_call x1, Pallas kernels: 16.3 us -> 10.1 us  [body(): pl.pallas_call(functools.partial(fields_kernel, members, most), grid=(ste...]
    pallas_call x1, Pallas kernels: 39.8 us -> 37.8 us  [observe(): pl.pallas_call(functools.partial(obs_kernel, axes, most), out_shape=[pltp...]
where the time goes in v4:
time: 108 us
  Pallas kernels  101 us (94%)
  local copies, waits for them, and re-layouts  3.55 us (3%)
  other arithmetic  3.08 us (3%)
    pallas_call x1, Pallas kernels, observe(): pl.pallas_call(functools.partial(obs_kernel, axes, most), out_shape=[pltp...  37.8 us
    pallas_call x1, Pallas kernels, body(): pl.pallas_call(functools.partial(carry_x_kernel, cx), out_shape=pltpu.VME...  14.1 us
    pallas_call x1, Pallas kernels, body(): pl.pallas_call(transport_kernel, grid=(steps,), in_specs=[levels_second(c...  10.7 us
    pallas_call x1, Pallas kernels, body(): pl.pallas_call(functools.partial(fields_kernel, members, most), grid=(ste...  10.1 us
    pallas_call x1, Pallas kernels, body(): pl.pallas_call(functools.partial(carry_y_kernel, cy), out_shape=[pltpu.VM...  7.6 us
    pallas_call x1, Pallas kernels, body(): pl.pallas_call(halo_kernel, out_shape=edge_shapes(1, lev, cx, cy), in_spe...  7.04 us
    pallas_call x1, Pallas kernels, body(): pl.pallas_call(functools.partial(rows_kernel, fields), grid=(steps,), in_...  6.79 us
    pallas_call x1, Pallas kernels, body(): pl.pallas_call(functools.partial(final_kernel, members), grid=(steps,), i...  6.55 us

profile of v4, /device:TPU:0, one launch (start us, length us, event | category | flops | bytes accessed | tf_op | source)
XLA Modules:
  0.0 108.1 jit_solution(9759772872015256613)
XLA Ops:
  0.6 0.0 copy-start.1
  0.6 0.9 convert_reduce_fusion
  1.6 0.7 multiply_add_fusion
  2.2 0.8 select_reduce_fusion
  3.0 0.7 sqrt_multiply_fusion
  3.7 0.1 stack.26
  3.8 0.1 stack.25
  3.9 0.1 stack.24
  4.0 0.1 broadcast_bitcast_fusion.coef_ref
  4.1 0.1 broadcast_in_dim.42.coef_ref
  4.2 1.0 copy.16
  5.2 0.0 copy-start
  5.2 0.0 copy-start.2
  5.2 1.5 %copy.20 = bf16[64,48,128]{2,0,1:T(8,128)(2,1)S(1)} copy(bf16[64,48,128]{2,1,0:T(8,128)(2,1)} %param.11) | data formatting | bytes 1572864 | tf_op args[0]
  6.7 0.0 copy-start.3
  6.7 0.7 copy-done.3
  7.4 37.8 %observe.1 = (f32[64,64,128]{2,1,0:T(8,128)S(1)}, s32[32,1,128]{2,1,0:T(1,128)S(1)}) custom-call(s32[64]{0:T(128)S(1)} %get-tuple-element.42.order_ref, s32[64]{0:T(128)S(1)} %get-tuple-element.41.line_ref, s32[64]{0:T(128)S(1)} %get-tuple-element.40.count_ref, bf16[512,64]{1,0:T(8,128)(2,1)S(1)} %bitcast.14, f32[1,512]{1,0:T(1,128)S(1)} %copy-done.3, ...), custom_call_target="tpu_custom_call" | custom-call | tf_op jit(solution)/shard_map/observe/pallas_call | solution.py:278
  45.2 0.0 copy-done.1
  45.2 0.0 copy-done
  45.2 0.0 copy-done.2
  45.2 10.1 %fields.1 = (f32[15360,128]{1,0:T(8,128)S(1)}, bf16[8,10,8,128]{3,2,1,0:T(8,128)(2,1)S(1)}, bf16[48,64,128]{2,1,0:T(8,128)(2,1)S(1)}, bf16[48,64,128]{2,1,0:T(8,...) custom-call(s32[32,1,128]{2,1,0:T(1,128)S(1)} %get-tuple-element.21.note_ref, ...), custom_call_target="tpu_custom_call" | custom-call | tf_op jit(solution)/shard_map/fields/pallas_call | solution.py:866
  55.3 14.1 %carry_x.1.enter_ref = f32[10,64,128]{2,1,0:T(8,128)S(1)} custom-call(bf16[8,10,8,128]{3,2,1,0:T(8,128)(2,1)S(1)} %get-tuple-element.24.s_ref, f32[8,3,8,128]{3,2,1,0:T(8,128)S(1)} %broadcast_bitcast_fusion.coef_ref), custom_call_target="tpu_custom_call" | custom-call | tf_op jit(solution)/shard_map/carry_x/pallas_call | solution.py:906
  69.4 6.8 %rows.1 = (f32[64,240,128]{2,1,0:T(8,128)S(1)}, bf16[2,64,240]{2,1,0:T(8,128)(2,1)S(1)}) custom-call(f32[64,240,128]{2,1,0:T(8,128)S(1)} %bitcast.12, f32[10,64,128]{2,1,0:T(8,128)S(1)} %carry_x.1.enter_ref, f32[3,64,128]{2,1,0:T(8,128)S(1)} %broadcast_in_dim.42.coef_ref), custom_call_target="tpu_custom_call" | custom-call | tf_op jit(solution)/shard_map/rows/pallas_call | solution.py:919
  76.2 7.6 %carry_y.1 = (f32[2,64,240]{2,1,0:T(8,128)S(1)}, bf16[2,2,3,64,128]{4,3,2,1,0:T(8,128)(2,1)S(1)}, bf16[3,2,54,8,128]{4,3,2,1,0:T(8,128)(2,1)S(1)}) custom-call(bf16[2,64,240]{2,1,0:T(8,128)(2,1)S(1)} %get-tuple-element.26.s_ref, f32[3,64,128]{2,1,0:T(8,128)S(1)} %broadcast_in_dim.42.coef_ref, bf16[2,2,3,64,128]{4,3,2,1,0:T(8,128)(2,1)S(1)} %get-tuple-element.27.edge_ref, ...), custom_call_target="tpu_custom_call" | custom-call | tf_op jit(solution)/shard_map/carry_y/pallas_call | solution.py:937
  83.8 6.6 %final.1 = (f32[4,64,48,128]{3,2,1,0:T(8,128)}, f32[48,64,128]{2,1,0:T(8,128)S(1)}, bf16[2,1,3,64,128]{4,3,2,1,0:T(8,128)(2,1)S(1)}, bf16[1,48,8,128]{3,2,1,0:T(8,128)(2,1)S(1)}) custom-call(f32[64,240,128]{2,1,0:T(8,128)S(1)} %get-tuple-element.25.z_ref, f32[2,64,240]{2,1,0:T(8,128)S(1)} %get-tuple-element.29.y_ref, f32[3,64,128]{2,1,0:T(8,128)S(1)} %broadcast_in_dim.42.coef_ref), custom_call_target="tpu_custom_call" | custom-call | tf_op jit(solution)/shard_map/final/pallas_call | solution.py:954
  90.4 7.0 %halo.1 = (bf16[2,1,3,64,128]{4,3,2,1,0:T(8,128)(2,1)S(1)}, bf16[3,1,54,8,128]{4,3,2,1,0:T(8,128)(2,1)S(1)}) custom-call(bf16[2,1,3,64,128]{4,3,2,1,0:T(8,128)(2,1)S(1)} %get-tuple-element.34.edge_ref, bf16[1,48,8,128]{3,2,1,0:T(8,128)(2,1)S(1)} %get-tuple-element.35.strip_ref), custom_call_target="tpu_custom_call" | custom-call | tf_op jit(solution)/shard_map/halo/pallas_call | solution.py:979
  97.4 10.7 %transport.1 = f32[3072,128]{1,0:T(8,128)} custom-call(f32[48,64,128]{2,1,0:T(8,128)S(1)} %get-tuple-element.31.s_ref, bf16[48,64,128]{2,1,0:T(8,128)(2,1)S(1)} %get-tuple-element.32.ut_ref, bf16[48,64,128]{2,1,0:T(8,128)(2,1)S(1)} %get-tuple-element.33.vt_ref, bf16[2,1,3,64,128]{4,3,2,1,0:T(8,128)(2,1)S(1)} %get-tuple-element.36.srow_ref, ...), custom_call_target="tpu_custom_call" | custom-call | tf_op jit(solution)/shard_map/transport/pallas_call | solution.py:995
  (5 shorter events, 0.1 us)
Async XLA Ops:
  0.6 44.6 %copy-start.1 = (bf16[64,48,128]{2,1,0:T(8,128)(2,1)S(1)}, bf16[64,48,128]{2,1,0:T(8,128)(2,1)}, u32[]{:S(2)}) copy-start(bf16[64,48,128]{2,1,0:T(8,128)(2,1)} %u_ref.1) | copy-start | bytes 2359300
  5.2 40.1 %copy-start = (bf16[4,64,48,128]{3,2,1,0:T(8,128)(2,1)S(1)}, bf16[4,64,48,128]{3,2,1,0:T(8,128)(2,1)}, u32[]{:S(2)}) copy-start(bf16[4,64,48,128]{3,2,1,0:T(8,128)(2,1)} %e_ref.1) | copy-start | bytes 9437188
  5.2 40.1 %copy-start.2 = (bf16[64,48,128]{2,1,0:T(8,128)(2,1)S(1)}, bf16[64,48,128]{2,1,0:T(8,128)(2,1)}, u32[]{:S(2)}) copy-start(bf16[64,48,128]{2,1,0:T(8,128)(2,1)} %v_ref.1) | copy-start | bytes 2359300
  6.7 0.7 copy-start.3
